TPU v7x, 256 devices: a whole 4x4x8 slice. The times are simulated.
256 devices in a mesh: dp: 16 (over y_lo, x, core), ctx: 16 (over y_hi, z).
Axes of the slice: x: 4, y: 4 (y_hi: 2, y_lo: 2; y = y_hi * 2 + y_lo), z: 8, core: 2. Of those that a mesh axis runs over, the one named last changes fastest.
Arguments:
- roll_query: bfloat16 [16, 2048, 4096], P('dp', 'ctx'), may hold values from -12 to 12
- roll_keys: bfloat16 [16, 2048, 512], P('dp', 'ctx'), may hold values from -12 to 12
- roll_values: bfloat16 [16, 2048, 512], P('dp', 'ctx'), may hold values from -6 to 6
- pack_dest: int32 [16, 256], P(None, 'ctx'), may hold values from 0 to 15, as said below
- segment_ids: int32 [16, 2048], P('dp', 'ctx'), may hold values from 0 to 15, never falling along the last dimension, each value on 1 to 1024 neighbouring positions
- reward_bins: int32 [16, 16], P('dp'), may hold values from 0 to 511
- reward_weight: float32 [4096], replicated, may hold values from -0.5 to 0.5
Outputs:
- attention_out: bfloat16 [16, 2048, 4096], P('dp', 'ctx')
- reward_hist: float32 [512], replicated
Inputs may be any that keep to these rules, and one draw needn't show every extreme that they name: For every column j the entries pack_dest[s, j] over s are a permutation of the packed sequences. Among the 16 columns of one ctx shard, at most 1 block go from one source to one packed sequence, and exactly 1 for some pair in every shard.
All inputs are finite; a program needn't handle non-finite values.
Results may differ from a plain program's by a relative error of at most 0.004.
Values may be sent and summed in bfloat16 or wider, within the bound.
A program may use at most 64 MiB of HBM per device.

v0:
```python
import math

import jax
import jax.numpy as jnp
from jax import lax
from jax.sharding import PartitionSpec as P

HQ = 32
HK = 4
HD = 128
BLK = 8
SEGS = 16
BINS = 512


NEG = -1e30


def shifted(block, axis, distance):
    devices = range(lax.axis_size(axis))
    route = [(i - distance, i) for i in devices if i - distance in devices]
    return lax.ppermute(block, axis, route)


def block_rank(labels):
    count_all = labels.shape[0]
    earlier = jnp.arange(count_all)[:, None] < jnp.arange(count_all)[None, :]
    same_label = labels[:, None] == labels[None, :]
    return jnp.sum(jnp.where(same_label & earlier, 1, 0), axis=0).astype(jnp.int32)


def select_rows(selector, source_rows):
    flat_rows = source_rows.reshape(selector.shape[1], -1)
    return jnp.dot(selector, flat_rows, preferred_element_type=jnp.float32).astype(jnp.bfloat16)


def local(roll_query, roll_keys, roll_values, pack_dest, segment_ids, reward_bins, reward_weight):
    dp_count = lax.axis_size("dp")
    dp_self = lax.axis_index("dp")
    ctx_self = lax.axis_index("ctx")
    row_count = roll_query.shape[1]
    block_count = row_count // BLK
    q_width = roll_query.shape[2]
    kv_width = roll_keys.shape[2]
    cap_here = (block_count + dp_count - 1) // dp_count
    slot_count = dp_count * cap_here
    group_size = HQ // HK
    score_scale = 1.0 / math.sqrt(HD)
    own_dest = lax.dynamic_index_in_dim(pack_dest, dp_self, 0, keepdims=False)
    send_slot = own_dest * cap_here + block_rank(own_dest)
    send_sel = (jnp.arange(slot_count, dtype=jnp.int32)[:, None] == send_slot[None, :]).astype(
        jnp.bfloat16
    )
    send_query = select_rows(send_sel, roll_query[0]).reshape(dp_count, cap_here * BLK, q_width)
    send_keys = select_rows(send_sel, roll_keys[0]).reshape(dp_count, cap_here * BLK, kv_width)
    send_values = select_rows(send_sel, roll_values[0]).reshape(dp_count, cap_here * BLK, kv_width)
    got_query, got_keys, got_values = (
        lax.all_to_all(send_query, "dp", split_axis=0, concat_axis=0, tiled=True),
        lax.all_to_all(send_keys, "dp", split_axis=0, concat_axis=0, tiled=True),
        lax.all_to_all(send_values, "dp", split_axis=0, concat_axis=0, tiled=True),
    )
    matched = pack_dest == dp_self
    earlier = jnp.arange(block_count)[:, None] < jnp.arange(block_count)[None, :]
    recv_rank = jnp.sum(jnp.where(matched[:, :, None] & earlier[None], 1, 0), axis=1)
    source_ids = jnp.arange(dp_count, dtype=jnp.int32)[:, None]
    recv_slot = jnp.sum(jnp.where(matched, source_ids * cap_here + recv_rank, 0), axis=0)
    recv_sel = (recv_slot[:, None] == jnp.arange(slot_count, dtype=jnp.int32)[None, :]).astype(
        jnp.bfloat16
    )
    packed_query = select_rows(recv_sel, got_query).reshape(row_count, q_width)
    packed_keys = select_rows(recv_sel, got_keys).reshape(row_count, kv_width)
    packed_values = select_rows(recv_sel, got_values).reshape(row_count, kv_width)
    seg_local = segment_ids[0]
    query_heads = packed_query.reshape(row_count, HK, group_size, HD)
    query_pos = ctx_self * row_count + jnp.arange(row_count, dtype=jnp.int32)

    def attend_block(running, key_rows, value_rows, key_segments, first_row):
        key_count = key_rows.shape[0]
        key_pos = first_row + jnp.arange(key_count, dtype=jnp.int32)
        allowed = (seg_local[:, None] == key_segments[None, :]) & (
            key_pos[None, :] <= query_pos[:, None]
        )
        scores = (
            jnp.einsum(
                "qgjd,kgd->gjqk",
                query_heads,
                key_rows.reshape(key_count, HK, HD),
                preferred_element_type=jnp.float32,
            )
            * score_scale
        )
        scores = jnp.where(allowed, scores, NEG)
        run_max, run_sum, run_acc = running
        new_max = jnp.maximum(run_max, jnp.max(scores, axis=-1))
        weights = jnp.where(allowed, jnp.exp(scores - new_max[..., None]), 0.0)
        shrink = jnp.exp(run_max - new_max)
        new_sum = run_sum * shrink + jnp.sum(weights, axis=-1)
        update = jnp.einsum(
            "gjqk,kgd->qgjd",
            weights.astype(jnp.bfloat16),
            value_rows.reshape(key_count, HK, HD),
            preferred_element_type=jnp.float32,
        )
        new_acc = run_acc * jnp.transpose(shrink, (2, 0, 1))[..., None] + update
        return (new_max, new_sum, new_acc)

    initial = (
        jnp.full((HK, group_size, row_count), NEG, jnp.float32),
        jnp.zeros((HK, group_size, row_count), jnp.float32),
        jnp.zeros((row_count, HK, group_size, HD), jnp.float32),
    )
    key_rows = lax.all_gather(packed_keys, "ctx", axis=0, tiled=True)
    value_rows = lax.all_gather(packed_values, "ctx", axis=0, tiled=True)
    key_segments = lax.all_gather(seg_local, "ctx", axis=0, tiled=True)
    key_count = key_rows.shape[0]

    def sub_block(turn_index, carried):
        offset = turn_index * row_count
        return attend_block(
            carried,
            lax.dynamic_slice_in_dim(key_rows, offset, row_count, 0),
            lax.dynamic_slice_in_dim(value_rows, offset, row_count, 0),
            lax.dynamic_slice_in_dim(key_segments, offset, row_count, 0),
            offset,
        )

    final_max, final_sum, final_acc = lax.fori_loop(0, key_count // row_count, sub_block, initial)
    attended = (
        (final_acc / jnp.transpose(final_sum, (2, 0, 1))[..., None])
        .reshape(row_count, q_width)
        .astype(jnp.bfloat16)
    )
    next_first = shifted(seg_local[:1] + 1, "ctx", -1)
    next_plus = jnp.concatenate([seg_local[1:] + 1, next_first])
    is_end = next_plus != seg_local + 1
    row_reward = jnp.dot(
        attended, reward_weight, precision=lax.Precision.HIGHEST, preferred_element_type=jnp.float32
    )
    kept = jnp.where(is_end, row_reward, 0.0)
    seg_match = seg_local[:, None] == jnp.arange(SEGS, dtype=jnp.int32)[None, :]
    bin_of = jnp.sum(jnp.where(seg_match, reward_bins[0][None, :], 0), axis=1)
    bin_match = bin_of[:, None] == jnp.arange(BINS, dtype=jnp.int32)[None, :]
    local_hist = jnp.sum(jnp.where(bin_match, kept[:, None], 0.0), axis=0)
    histogram = lax.psum(local_hist, ("dp", "ctx"))
    return (attended.reshape(1, row_count, q_width), histogram)


def solution(mesh):
    in_specs = (
        P("dp", "ctx", None),
        P("dp", "ctx", None),
        P("dp", "ctx", None),
        P(None, "ctx"),
        P("dp", "ctx"),
        P("dp", None),
        P(),
    )
    out_specs = (P("dp", "ctx", None), P())
    return jax.shard_map(local, mesh=mesh, in_specs=in_specs, out_specs=out_specs, check_vma=False)
```

profile of v0, /device:TPU:24, one launch (start us, length us, event | category | flops | bytes accessed | tf_op | source)
XLA Modules:
  0.0 374.6 jit_solution(7069641416522338953)
XLA Ops:
  10.6 5.8 %all-to-all-start = ((bf16[16,8,512]{2,1,0:T(8,128)(2,1)}), bf16[16,8,512]{2,1,0:T(8,128)(2,1)S(1)}, u32[]{:S(2)}, u32[]{:S(2)}) async-start(bf16[16,8,512]{2,1,0:T(8,128)(2,1)} %bitcast.28), calls=%async_computation | async-start | bytes 262144 | tf_op jit(solution)/shard_map/all_to_all | solution.py:59
  17.9 3.5 all-to-all-done
  22.9 9.0 %all_to_all.15 = bf16[16,8,512]{2,1,0:T(8,128)(2,1)S(1)} all-to-all(bf16[16,8,512]{2,1,0:T(8,128)(2,1)S(1)} %bitcast.106), channel_id=1, replica_groups=mesh['dp'=16,'ctx'=16] {'dp'}, dimensions={0} | all-to-all | bytes 262144 | tf_op jit(solution)/shard_map/all_to_all | solution.py:60
  34.1 1.5 copy.33
  35.7 4.9 %all-to-all-start.1 = ((bf16[16,8,4096]{2,1,0:T(8,128)(2,1)}), bf16[16,8,4096]{2,1,0:T(8,128)(2,1)S(1)}, u32[]{:S(2)}, u32[]{:S(2)}) async-start(bf16[16,8,4096]{2,1,0:T(8,128)(2,1)} %bitcast.32), calls=%async_computation.1 | async-start | bytes 2097152 | tf_op jit(solution)/shard_map/all_to_all | solution.py:58
  40.6 9.7 %collective-permute-start = (s32[1]{0:T(128)}, s32[1]{0:T(128)}, u32[]{:S(2)}, u32[]{:S(2)}) collective-permute-start(s32[1]{0:T(128)} %bitcast.9), channel_id=1, source_target_pairs={{1,0},{2,1},{3,2},{4,3},{5,4},{6,5},{7,6},{8,7},{9,8},{10,9},{11,1... | collective-permute-start | bytes 20 | tf_op jit(solution)/shard_map/ppermute | solution.py:22
  50.3 36.7 %all-gather = s32[1,2048]{1,0:T(1,128)S(1)} all-gather(s32[1,128]{1,0:T(1,128)S(1)} %copy-done.3), channel_id=2, replica_groups=mesh['dp'=16,'ctx'=16] {'ctx'}, dimensions={1}, use_global_device_ids=true | all-gather | bytes 8704 | tf_op jit(solution)/shard_map/all_gather | solution.py:114
  89.2 18.6 %all-gather.4.cloned.1.call-done = bf16[2048,512]{0,1:T(8,128)(2,1)} async-done(((bf16[128,512]{0,1:T(8,128)(2,1)}), bf16[2048,512]{0,1:T(8,128)(2,1)}) %all-gather.4.cloned.1.call-update) | async-done | bytes 2097168 | tf_op jit(solution)/shard_map/all_gather | solution.py:112
  107.8 84.1 %all-gather.6.cloned.1.call-done = bf16[2048,512]{0,1:T(8,128)(2,1)} async-done(((bf16[128,512]{0,1:T(8,128)(2,1)}), bf16[2048,512]{0,1:T(8,128)(2,1)}) %all-gather.6.cloned.1.call-update) | async-done | bytes 2097168 | tf_op jit(solution)/shard_map/all_gather | solution.py:113
  191.9 96.3 %while.18 = (s32[]{:T(128)}, f32[4,8,128]{2,1,0:T(8,128)S(1)}, f32[4,8,128]{2,1,0:T(8,128)S(1)}, f32[128,4,8,128]{0,3,2,1:T(8,128)}, s32[1,128]{1,0:T(1,128)S(1)...) while((s32[]{:T(128)}, f32[4,8,128]{2,1,0:T(8,128)S(1)}, ...), condition=%wide.region_6.7_spmd.clone, body=%wide.region_3.6_spmd.clone.sunk | while | flops 276898048 | bytes 12652751 | solution.py:127
  192.1 1.0 constant_dynamic-slice_fusion.4
  193.7 2.2 bitcast_add_fusion.3
  196.6 1.0 constant_dynamic-slice_fusion.4
  198.2 3.8 %bitcast_add_fusion.3 = f32[128,4,8,128]{0,3,2,1:T(8,128)} fusion(f32[128,4,8,128]{0,3,2,1:T(8,128)} %get-tuple-element.362, bf16[128,4,128,1]{0,2,3,1:T(8,128)(2,1)S(1)} %bitcast.94, f32[4,128,128,8]{2,1,3,0:T(8,128)S(1)} %get-tuple-element.342, f32[128,4,8]{0,2,1:T(8,128)S(1)} %get-tuple-element.344, f32[4,8,128]{2,1,0:T(8,128)S(1)} %get-tuple-element.374, ...), kind=kOutput, calls=%fused_computation.1.clone.1 | convolution fusion | flops 138412032 | bytes 6471681 | tf_op jit(solution)/shard_map/while/body/eval_jaxpr/gjqk,kgd->qgjd/dot_general | solution.py:98
  204.3 3.8 %bitcast_add_fusion.3 = f32[128,4,8,128]{0,3,2,1:T(8,128)} fusion(f32[128,4,8,128]{0,3,2,1:T(8,128)} %get-tuple-element.362, bf16[128,4,128,1]{0,2,3,1:T(8,128)(2,1)S(1)} %bitcast.94, f32[4,128,128,8]{2,1,3,0:T(8,128)S(1)} %get-tuple-element.342, f32[128,4,8]{0,2,1:T(8,128)S(1)} %get-tuple-element.344, f32[4,8,128]{2,1,0:T(8,128)S(1)} %get-tuple-element.374, ...), kind=kOutput, calls=%fused_computation.1.clone.1 | convolution fusion | flops 138412032 | bytes 6471681 | tf_op jit(solution)/shard_map/while/body/eval_jaxpr/gjqk,kgd->qgjd/dot_general | solution.py:98
  210.4 3.8 %bitcast_add_fusion.3 = f32[128,4,8,128]{0,3,2,1:T(8,128)} fusion(f32[128,4,8,128]{0,3,2,1:T(8,128)} %get-tuple-element.362, bf16[128,4,128,1]{0,2,3,1:T(8,128)(2,1)S(1)} %bitcast.94, f32[4,128,128,8]{2,1,3,0:T(8,128)S(1)} %get-tuple-element.342, f32[128,4,8]{0,2,1:T(8,128)S(1)} %get-tuple-element.344, f32[4,8,128]{2,1,0:T(8,128)S(1)} %get-tuple-element.374, ...), kind=kOutput, calls=%fused_computation.1.clone.1 | convolution fusion | flops 138412032 | bytes 6471681 | tf_op jit(solution)/shard_map/while/body/eval_jaxpr/gjqk,kgd->qgjd/dot_general | solution.py:98
  216.5 3.8 %bitcast_add_fusion.3 = f32[128,4,8,128]{0,3,2,1:T(8,128)} fusion(f32[128,4,8,128]{0,3,2,1:T(8,128)} %get-tuple-element.362, bf16[128,4,128,1]{0,2,3,1:T(8,128)(2,1)S(1)} %bitcast.94, f32[4,128,128,8]{2,1,3,0:T(8,128)S(1)} %get-tuple-element.342, f32[128,4,8]{0,2,1:T(8,128)S(1)} %get-tuple-element.344, f32[4,8,128]{2,1,0:T(8,128)S(1)} %get-tuple-element.374, ...), kind=kOutput, calls=%fused_computation.1.clone.1 | convolution fusion | flops 138412032 | bytes 6471681 | tf_op jit(solution)/shard_map/while/body/eval_jaxpr/gjqk,kgd->qgjd/dot_general | solution.py:98
  222.7 3.8 %bitcast_add_fusion.3 = f32[128,4,8,128]{0,3,2,1:T(8,128)} fusion(f32[128,4,8,128]{0,3,2,1:T(8,128)} %get-tuple-element.362, bf16[128,4,128,1]{0,2,3,1:T(8,128)(2,1)S(1)} %bitcast.94, f32[4,128,128,8]{2,1,3,0:T(8,128)S(1)} %get-tuple-element.342, f32[128,4,8]{0,2,1:T(8,128)S(1)} %get-tuple-element.344, f32[4,8,128]{2,1,0:T(8,128)S(1)} %get-tuple-element.374, ...), kind=kOutput, calls=%fused_computation.1.clone.1 | convolution fusion | flops 138412032 | bytes 6471681 | tf_op jit(solution)/shard_map/while/body/eval_jaxpr/gjqk,kgd->qgjd/dot_general | solution.py:98
  228.8 3.8 %bitcast_add_fusion.3 = f32[128,4,8,128]{0,3,2,1:T(8,128)} fusion(f32[128,4,8,128]{0,3,2,1:T(8,128)} %get-tuple-element.362, bf16[128,4,128,1]{0,2,3,1:T(8,128)(2,1)S(1)} %bitcast.94, f32[4,128,128,8]{2,1,3,0:T(8,128)S(1)} %get-tuple-element.342, f32[128,4,8]{0,2,1:T(8,128)S(1)} %get-tuple-element.344, f32[4,8,128]{2,1,0:T(8,128)S(1)} %get-tuple-element.374, ...), kind=kOutput, calls=%fused_computation.1.clone.1 | convolution fusion | flops 138412032 | bytes 6471681 | tf_op jit(solution)/shard_map/while/body/eval_jaxpr/gjqk,kgd->qgjd/dot_general | solution.py:98
  234.9 3.8 %bitcast_add_fusion.3 = f32[128,4,8,128]{0,3,2,1:T(8,128)} fusion(f32[128,4,8,128]{0,3,2,1:T(8,128)} %get-tuple-element.362, bf16[128,4,128,1]{0,2,3,1:T(8,128)(2,1)S(1)} %bitcast.94, f32[4,128,128,8]{2,1,3,0:T(8,128)S(1)} %get-tuple-element.342, f32[128,4,8]{0,2,1:T(8,128)S(1)} %get-tuple-element.344, f32[4,8,128]{2,1,0:T(8,128)S(1)} %get-tuple-element.374, ...), kind=kOutput, calls=%fused_computation.1.clone.1 | convolution fusion | flops 138412032 | bytes 6471681 | tf_op jit(solution)/shard_map/while/body/eval_jaxpr/gjqk,kgd->qgjd/dot_general | solution.py:98
  241.0 3.8 %bitcast_add_fusion.3 = f32[128,4,8,128]{0,3,2,1:T(8,128)} fusion(f32[128,4,8,128]{0,3,2,1:T(8,128)} %get-tuple-element.362, bf16[128,4,128,1]{0,2,3,1:T(8,128)(2,1)S(1)} %bitcast.94, f32[4,128,128,8]{2,1,3,0:T(8,128)S(1)} %get-tuple-element.342, f32[128,4,8]{0,2,1:T(8,128)S(1)} %get-tuple-element.344, f32[4,8,128]{2,1,0:T(8,128)S(1)} %get-tuple-element.374, ...), kind=kOutput, calls=%fused_computation.1.clone.1 | convolution fusion | flops 138412032 | bytes 6471681 | tf_op jit(solution)/shard_map/while/body/eval_jaxpr/gjqk,kgd->qgjd/dot_general | solution.py:98
  247.2 3.8 %bitcast_add_fusion.3 = f32[128,4,8,128]{0,3,2,1:T(8,128)} fusion(f32[128,4,8,128]{0,3,2,1:T(8,128)} %get-tuple-element.362, bf16[128,4,128,1]{0,2,3,1:T(8,128)(2,1)S(1)} %bitcast.94, f32[4,128,128,8]{2,1,3,0:T(8,128)S(1)} %get-tuple-element.342, f32[128,4,8]{0,2,1:T(8,128)S(1)} %get-tuple-element.344, f32[4,8,128]{2,1,0:T(8,128)S(1)} %get-tuple-element.374, ...), kind=kOutput, calls=%fused_computation.1.clone.1 | convolution fusion | flops 138412032 | bytes 6471681 | tf_op jit(solution)/shard_map/while/body/eval_jaxpr/gjqk,kgd->qgjd/dot_general | solution.py:98
  253.3 3.8 %bitcast_add_fusion.3 = f32[128,4,8,128]{0,3,2,1:T(8,128)} fusion(f32[128,4,8,128]{0,3,2,1:T(8,128)} %get-tuple-element.362, bf16[128,4,128,1]{0,2,3,1:T(8,128)(2,1)S(1)} %bitcast.94, f32[4,128,128,8]{2,1,3,0:T(8,128)S(1)} %get-tuple-element.342, f32[128,4,8]{0,2,1:T(8,128)S(1)} %get-tuple-element.344, f32[4,8,128]{2,1,0:T(8,128)S(1)} %get-tuple-element.374, ...), kind=kOutput, calls=%fused_computation.1.clone.1 | convolution fusion | flops 138412032 | bytes 6471681 | tf_op jit(solution)/shard_map/while/body/eval_jaxpr/gjqk,kgd->qgjd/dot_general | solution.py:98
  259.4 3.8 %bitcast_add_fusion.3 = f32[128,4,8,128]{0,3,2,1:T(8,128)} fusion(f32[128,4,8,128]{0,3,2,1:T(8,128)} %get-tuple-element.362, bf16[128,4,128,1]{0,2,3,1:T(8,128)(2,1)S(1)} %bitcast.94, f32[4,128,128,8]{2,1,3,0:T(8,128)S(1)} %get-tuple-element.342, f32[128,4,8]{0,2,1:T(8,128)S(1)} %get-tuple-element.344, f32[4,8,128]{2,1,0:T(8,128)S(1)} %get-tuple-element.374, ...), kind=kOutput, calls=%fused_computation.1.clone.1 | convolution fusion | flops 138412032 | bytes 6471681 | tf_op jit(solution)/shard_map/while/body/eval_jaxpr/gjqk,kgd->qgjd/dot_general | solution.py:98
  265.5 3.8 %bitcast_add_fusion.3 = f32[128,4,8,128]{0,3,2,1:T(8,128)} fusion(f32[128,4,8,128]{0,3,2,1:T(8,128)} %get-tuple-element.362, bf16[128,4,128,1]{0,2,3,1:T(8,128)(2,1)S(1)} %bitcast.94, f32[4,128,128,8]{2,1,3,0:T(8,128)S(1)} %get-tuple-element.342, f32[128,4,8]{0,2,1:T(8,128)S(1)} %get-tuple-element.344, f32[4,8,128]{2,1,0:T(8,128)S(1)} %get-tuple-element.374, ...), kind=kOutput, calls=%fused_computation.1.clone.1 | convolution fusion | flops 138412032 | bytes 6471681 | tf_op jit(solution)/shard_map/while/body/eval_jaxpr/gjqk,kgd->qgjd/dot_general | solution.py:98
  271.6 3.8 %bitcast_add_fusion.3 = f32[128,4,8,128]{0,3,2,1:T(8,128)} fusion(f32[128,4,8,128]{0,3,2,1:T(8,128)} %get-tuple-element.362, bf16[128,4,128,1]{0,2,3,1:T(8,128)(2,1)S(1)} %bitcast.94, f32[4,128,128,8]{2,1,3,0:T(8,128)S(1)} %get-tuple-element.342, f32[128,4,8]{0,2,1:T(8,128)S(1)} %get-tuple-element.344, f32[4,8,128]{2,1,0:T(8,128)S(1)} %get-tuple-element.374, ...), kind=kOutput, calls=%fused_computation.1.clone.1 | convolution fusion | flops 138412032 | bytes 6471681 | tf_op jit(solution)/shard_map/while/body/eval_jaxpr/gjqk,kgd->qgjd/dot_general | solution.py:98
  277.8 3.8 %bitcast_add_fusion.3 = f32[128,4,8,128]{0,3,2,1:T(8,128)} fusion(f32[128,4,8,128]{0,3,2,1:T(8,128)} %get-tuple-element.362, bf16[128,4,128,1]{0,2,3,1:T(8,128)(2,1)S(1)} %bitcast.94, f32[4,128,128,8]{2,1,3,0:T(8,128)S(1)} %get-tuple-element.342, f32[128,4,8]{0,2,1:T(8,128)S(1)} %get-tuple-element.344, f32[4,8,128]{2,1,0:T(8,128)S(1)} %get-tuple-element.374, ...), kind=kOutput, calls=%fused_computation.1.clone.1 | convolution fusion | flops 138412032 | bytes 6471681 | tf_op jit(solution)/shard_map/while/body/eval_jaxpr/gjqk,kgd->qgjd/dot_general | solution.py:98
  283.9 3.8 %bitcast_add_fusion.3 = f32[128,4,8,128]{0,3,2,1:T(8,128)} fusion(f32[128,4,8,128]{0,3,2,1:T(8,128)} %get-tuple-element.362, bf16[128,4,128,1]{0,2,3,1:T(8,128)(2,1)S(1)} %bitcast.94, f32[4,128,128,8]{2,1,3,0:T(8,128)S(1)} %get-tuple-element.342, f32[128,4,8]{0,2,1:T(8,128)S(1)} %get-tuple-element.344, f32[4,8,128]{2,1,0:T(8,128)S(1)} %get-tuple-element.374, ...), kind=kOutput, calls=%fused_computation.1.clone.1 | convolution fusion | flops 138412032 | bytes 6471681 | tf_op jit(solution)/shard_map/while/body/eval_jaxpr/gjqk,kgd->qgjd/dot_general | solution.py:98
  288.2 1.9 divide_convert_fusion
  290.1 1.3 copy.28
  291.4 1.1 compare_select_fusion
  292.7 75.1 %psum.7 = f32[512]{0:T(512)} all-reduce(f32[512]{0:T(512)S(1)} %select_reduce_fusion), channel_id=1, replica_groups=mesh['dp'=16,'ctx'=16] {'dp','ctx'}, use_global_device_ids=true, to_apply=%region_9.10 | all-reduce | flops 512 | bytes 4096 | tf_op jit(solution)/shard_map/psum | solution.py:144
  (191 shorter events, 45.4 us)
Async XLA Ops:
  7.2 284.3 %copy-start = (f32[4096]{0:T(1024)S(1)}, f32[4096]{0:T(1024)}, u32[]{:S(2)}) copy-start(f32[4096]{0:T(1024)} %param.15) | copy-start | bytes 49156
  7.2 15.5 %copy-start.2 = (bf16[1,128,512]{2,1,0:T(8,128)(2,1)S(1)}, bf16[1,128,512]{2,1,0:T(8,128)(2,1)}, u32[]{:S(2)}) copy-start(bf16[1,128,512]{2,1,0:T(8,128)(2,1)} %param.11) | copy-start | bytes 393220
  9.7 23.4 %copy-start.1 = (bf16[1,128,4096]{2,1,0:T(8,128)(2,1)S(1)}, bf16[1,128,4096]{2,1,0:T(8,128)(2,1)}, u32[]{:S(2)}) copy-start(bf16[1,128,4096]{2,1,0:T(8,128)(2,1)} %param.9) | copy-start | bytes 3145732
  10.6 10.9 %all-to-all-start = ((bf16[16,8,512]{2,1,0:T(8,128)(2,1)}), bf16[16,8,512]{2,1,0:T(8,128)(2,1)S(1)}, u32[]{:S(2)}, u32[]{:S(2)}) async-start(bf16[16,8,512]{2,1,0:T(8,128)(2,1)} %bitcast.28), calls=%async_computation | async-start | bytes 262144 | tf_op jit(solution)/shard_map/all_to_all | solution.py:59
  16.3 91.5 %all-gather.4.cloned.1.call-start = ((), (), s32[]{:S(2)}) async-start(), calls=%async_computation.3 | async-start | bytes 2228224 | tf_op jit(solution)/shard_map/all_gather | solution.py:112
  22.6 169.3 %all-gather.6.cloned.1.call-start = ((), (), s32[]{:S(2)}) async-start(), calls=%async_computation.4 | async-start | bytes 2228224 | tf_op jit(solution)/shard_map/all_gather | solution.py:113
  34.1 6.5 %copy-start.3 = (s32[1,128]{1,0:T(1,128)S(1)}, s32[1,128]{1,0:T(1,128)}, u32[]{:S(2)}) copy-start(s32[1,128]{1,0:T(1,128)} %param.13) | copy-start | bytes 1540
  34.1 52.9 %copy-start.4 = (s32[1,16]{1,0:T(1,128)S(1)}, s32[1,16]{1,0:T(1,128)}, u32[]{:S(2)}) copy-start(s32[1,16]{1,0:T(1,128)} %param.14) | copy-start | bytes 196
  35.7 51.5 %all-to-all-start.1 = ((bf16[16,8,4096]{2,1,0:T(8,128)(2,1)}), bf16[16,8,4096]{2,1,0:T(8,128)(2,1)S(1)}, u32[]{:S(2)}, u32[]{:S(2)}) async-start(bf16[16,8,4096]{2,1,0:T(8,128)(2,1)} %bitcast.32), calls=%async_computation.1 | async-start | bytes 2097152 | tf_op jit(solution)/shard_map/all_to_all | solution.py:58
  40.6 250.8 %collective-permute-start = (s32[1]{0:T(128)}, s32[1]{0:T(128)}, u32[]{:S(2)}, u32[]{:S(2)}) collective-permute-start(s32[1]{0:T(128)} %bitcast.9), channel_id=1, source_target_pairs={{1,0},{2,1},{3,2},{4,3},{5,4},{6,5},{7,6},{8,7},{9,8},{10,9},{11,1... | collective-permute-start | bytes 20 | tf_op jit(solution)/shard_map/ppermute | solution.py:22
Sparse Core Ops, SparseCore 0:
  22.7 85.0 all-gather.3
  110.3 81.5 all-gather.5
where the time goes:
time: 379 us; the launch traced here: 375 us
  blocking collectives  121 us (32%)
  waiting for transfers between devices  106 us (28%)
  matrix products  69.7 us (18%)
  local copies, waits for them, and re-layouts  26.4 us (7%)
  starting transfers between devices  20.5 us (5%)
  other arithmetic  15.5 us (4%)
  between operations  14.3 us (4%)
    all_gather x1, waiting for transfers between devices, local(): value_rows = lax.all_gather(packed_values, 'ctx', axis=0, tiled=True)  84.1 us
    psum x1, blocking collectives, local(): histogram = lax.psum(local_hist, ('dp', 'ctx'))  75.1 us
    dot_general x16, matrix products, attend_block(): jnp.einsum('gjqk,kgd->qgjd', weights.astype(jnp.bfloat16), value_rows.res...  58.5 us
    all_gather x1, blocking collectives, local(): key_segments = lax.all_gather(seg_local, 'ctx', axis=0, tiled=True)  36.7 us
    all_gather x1, waiting for transfers between devices, local(): key_rows = lax.all_gather(packed_keys, 'ctx', axis=0, tiled=True)  18.6 us
    dynamic_slice x16, local copies, waits for them, and re-layouts, sub_block(): lax.dynamic_slice_in_dim(value_rows, offset, row_count, 0)  16 us
    ppermute x1, starting transfers between devices, shifted(): return lax.ppermute(block, axis, route)  9.72 us
    all_to_all x1, blocking collectives, local(): lax.all_to_all(send_values, 'dp', split_axis=0, concat_axis=0, tiled=True)  9.04 us
  transfers between devices with their start and end apart: 5, of which 3 were waited for; matrix products, arithmetic and copies ran while one was open for 28% of the time, Pallas kernels for 0%

commit v1 on v0

v1 whole, which is shorter than its diff:
```python
import functools
import math

import jax
import jax.numpy as jnp
from jax import lax
from jax.experimental import pallas as pl
from jax.experimental.pallas import tpu as pltpu
from jax.sharding import PartitionSpec as P

HQ = 32
HK = 4
HD = 128
TQ = 128
BLK = 8
NB = 16
SEGS = 16
BINS = 512
GROUP = HQ // HK
WIN = 9
NEG = -1e30
SCALE = math.log2(math.e) / math.sqrt(HD)
MESH = pl.DeviceIdType.MESH

ROUTES = (
    (264, 7, 1, 263, 8, 257, -2, 24, 23, -18, 279, -23, 360, -6, 88, -3, 39, -22, 344),
    (16, 274, 281, 18, 25, -1, 272, 2, -17, -20, 258, 313, -3, 32),
    (42, 291, 298, 35, -18, -20, 305, 275, -2, 33, 19, -1, 3, -17, 259),
    (315, 52, 306, 308, 59, -21, -19, 331, 292, -3, 36, -18, 276, -2, 20, -1, -17),
    (323, 76, 69, 332, 325, -4, 53, -20, -23, 364, 309, -19, 293, -3, 37, -18, -1, -2, -17),
    (86, 349, 93, 342, -23, -5, 356, 70, 365, -21, -24, 326, 381, -4, 54, -1, -20, 4, 310, -19, -17, 260, 294, -3, -2, 38, -18),
    (357, 110, 359, 103, 366, -24, -6, 373, 382, 87, -22, -1, 5, 343, -5, -17, 261, 71, -21, -2, 21, 327, -4, -18, 55, 277, -20, 311, -19, 295, -3),
    (374, 127, 383, -1, -23, 6, 352, -17, -7, 262, 111, -6, -2, 22, 80, -22, -18, 278, 336, -5, 79, -21, -4, -3, -20, -19),
    (399, 393, 143, 137, -10, -17, 159, -26, -1, 415, -18, -8, 121, -2, -24, -11, 175, 377, -23, -3, 361, -7, -20, 105, -6, -19, 89, -22, -4, -5, -21),
    (154, 152, 410, 408, -25, -18, -11, 280, 394, -9, -2, 138, 168, -3, 40, -19, -20, -8, 312, 122, -24, 378, 296, -4, -23, 56, 362, -21, -7, 328, -5, -6, -22),
    (427, 169, 171, -10, -3, 41, 155, -26, -19, 297, 411, -20, -25, 395, -9, -4, 57, 139, -21, 329, -5, -8, 123, 73, -24, -22, 345, -23, -7, -6),
    (188, 444, -27, -20, 314, 428, -11, -4, 172, 58, -10, -5, -21, 330, 156, -26, -22, 412, 74, -25, -6, 346, 396, -9, -7, 140, 106, -23, -8, 90, -24),
    (205, 461, -12, -5, 189, 75, -28, -21, 445, -22, -27, 347, 429, -11, -6, 91, -23, 173, -7, -10, 107, -26, -24, 363, -8, -25, 379, -9),
    (222, 478, -13, -22, 206, 348, -29, -6, 462, 92, -7, -12, -23, 190, 108, -28, -25, -24, 380, 446, -8, -27, 124, 430, -10, -11, -26, -9),
    (239, 495, -14, -7, 223, 109, -30, -23, -25, 479, 397, -13, -24, -8, 125, 207, -29, -10, 157, 463, -12, -26, 191, 413, -28, -9, 141, 447, -27, -11, 431),
    (-25, -15, 398, -8, 120, -31, -9, 126, -24, 376, -14, -10, 158, -30, -26, 414, -7, 104, -13, 142, -11, -29, 174, -5, -12, 72, -28, -27),
)


def remote(src, dst, send_sem, recv_sem, device_id):
    return pltpu.make_async_remote_copy(
        src_ref=src, dst_ref=dst, send_sem=send_sem, recv_sem=recv_sem, device_id=device_id, device_id_type=MESH
    )


def kernel(
    dest_ref, bins_ref, rq_ref, rk_ref, rv_ref, seg_ref, rw_ref,
    out_ref, hist_ref,
    qsend, qrecv, kvsend, kvrecv, qs, kv, segbuf, bias, racc, hist_a, hist_b,
    q_ss, q_rs, kv_ss, kv_rs, seg_ss, seg_rs, item_ss, item_rs, ha_ss, ha_rs, hb_ss, hb_rs,
):
    dp = lax.axis_index("dp")
    ctx = lax.axis_index("ctx")

    for b in range(1, WIN):
        @pl.when(b > ctx)
        def _():
            for h in range(2):
                kv[h, b] = jnp.zeros((HK, TQ, HD), jnp.bfloat16)

    barrier = pltpu.get_barrier_semaphore()

    def greet(k, carry):
        pl.semaphore_signal(barrier, inc=1, device_id={"dp": (dp + k) % 16}, device_id_type=MESH)
        pl.semaphore_signal(barrier, inc=1, device_id={"ctx": (ctx + k) % 16}, device_id_type=MESH)
        return carry

    lax.fori_loop(1, 16, greet, 0)

    def fill_kv(d, carry):
        inv = jnp.int32(0)
        for j in range(NB):
            inv = jnp.where(dest_ref[dp, j] == d, j, inv)
        kvsend[d, :, : HK * HD] = rk_ref[inv]
        kvsend[d, :, HK * HD :] = rv_ref[inv]
        return carry

    lax.fori_loop(0, NB, fill_kv, 0)
    pl.semaphore_wait(barrier, 30)

    def kv_copy(k):
        d = (dp + k) % 16
        return remote(kvsend.at[d], kvrecv.at[dp], kv_ss.at[k], kv_rs.at[dp], {"dp": d})

    def kv_start(k, carry):
        kv_copy(k).start()
        return carry

    lax.fori_loop(1, 16, kv_start, 0)
    kvrecv[dp] = kvsend[dp]
    segbuf[ctx] = seg_ref[0]

    def seg_copy(k):
        return remote(seg_ref.at[0], segbuf.at[ctx], seg_ss.at[k], seg_rs.at[ctx], {"ctx": (ctx + k) % 16})

    def seg_start(k, carry):
        seg_copy(k).start()
        return carry

    def fill_q(d, carry):
        inv = jnp.int32(0)
        for j in range(NB):
            inv = jnp.where(dest_ref[dp, j] == d, j, inv)
        qsend[d] = rq_ref[inv]
        return carry

    lax.fori_loop(0, NB, fill_q, 0)

    def q_copy(k):
        d = (dp + k) % 16
        return remote(qsend.at[d], qrecv.at[dp], q_ss.at[k], q_rs.at[dp], {"dp": d})

    def q_start(k, carry):
        q_copy(k).start()
        return carry

    def kv_wait(k, carry):
        s = (dp + k) % 16
        remote(kvsend.at[s], kvrecv.at[s], kv_ss.at[k], kv_rs.at[s], {"dp": s}).wait_recv()
        return carry

    lax.fori_loop(1, 16, kv_wait, 0)

    def source_of(j):
        src = jnp.int32(0)
        for s in range(16):
            src = jnp.where(dest_ref[s, j] == dp, s, src)
        return src

    def pack_kv(jj, carry):
        top = kvrecv[source_of(2 * jj)].astype(jnp.float32)
        low = kvrecv[source_of(2 * jj + 1)].astype(jnp.float32)
        rows = jnp.concatenate([top, low], axis=0).astype(jnp.bfloat16)
        at = pl.ds(pl.multiple_of(jj * 16, 16), 16)
        for h in range(2):
            for g in range(HK):
                lane = (h * HK + g) * HD
                kv[h, ctx, g, at, :] = rows[:, lane : lane + HD]
        return carry

    lax.fori_loop(0, NB // 2, pack_kv, 0)

    def item_copy(h, b, to, slot):
        return remote(kv.at[h, b], kv.at[h, b], item_ss.at[slot], item_rs.at[h * 16 + b], {"ctx": to})

    def run_steps(steps, slot):
        for n in steps:
            if n < 0:
                item = -1 - n
                item_copy(item // 16, item % 16, ctx, 0).wait_recv()
            else:
                item = n // 16
                item_copy(item // 16, item % 16, n % 16, slot).start()
                slot += 1
        return slot

    first = [next((i for i, n in enumerate(steps) if n < 0), len(steps)) for steps in ROUTES]
    for c, steps in enumerate(ROUTES):
        @pl.when(ctx == c)
        def _():
            run_steps(steps[: first[c]], 0)

    lax.fori_loop(1, 16, q_start, 0)
    qrecv[dp] = qsend[dp]
    lax.fori_loop(1, 16, seg_start, 0)
    for c, steps in enumerate(ROUTES):
        @pl.when(ctx == c)
        def _():
            run_steps(steps[first[c] :], first[c])

    def q_wait(k, carry):
        s = (dp + k) % 16
        remote(qsend.at[s], qrecv.at[s], q_ss.at[k], q_rs.at[s], {"dp": s}).wait_recv()
        return carry

    lax.fori_loop(1, 16, q_wait, 0)

    def pack_q(jj, carry):
        top = qrecv[source_of(2 * jj)].astype(jnp.float32)
        low = qrecv[source_of(2 * jj + 1)].astype(jnp.float32)
        rows = jnp.concatenate([top, low], axis=0).astype(jnp.bfloat16)
        at = pl.ds(pl.multiple_of(jj * 16, 16), 16)
        for h in range(HQ):
            qs[h, at, :] = rows[:, h * HD : (h + 1) * HD]
        return carry

    lax.fori_loop(0, NB // 2, pack_q, 0)

    def seg_wait(k, carry):
        s = (ctx + k) % 16
        remote(seg_ref.at[0], segbuf.at[s], seg_ss.at[k], seg_rs.at[s], {"ctx": s}).wait_recv()
        return carry

    lax.fori_loop(1, 16, seg_wait, 0)

    def column(row):
        return jnp.transpose(jnp.broadcast_to(row.astype(jnp.float32), (TQ, TQ)))

    lane = lax.broadcasted_iota(jnp.int32, (TQ, TQ), 1)
    sub = lax.broadcasted_iota(jnp.int32, (TQ, TQ), 0)
    seg_row = seg_ref[0]
    seg_col = column(seg_row)
    base = jnp.maximum(ctx - (WIN - 1), 0)
    for w in range(WIN):
        keys = segbuf[base + w].astype(jnp.float32)
        allowed = (seg_col == keys) & ((base + w - ctx) * TQ + lane <= sub)
        bias[:, w * TQ : (w + 1) * TQ] = jnp.where(allowed, 0.0, NEG)

    racc[...] = jnp.zeros_like(racc)

    def heads(i, carry):
        per = 2
        g = i // (GROUP // per)
        q = qs[pl.ds(i * per, per)].reshape(per * TQ, HD)
        k = kv[0, pl.ds(base, WIN), g].reshape(WIN * TQ, HD)
        v = kv[1, pl.ds(base, WIN), g].reshape(WIN * TQ, HD)
        s = lax.dot_general(q, k, (((1,), (1,)), ((), ())), preferred_element_type=jnp.float32)
        s = (s * SCALE).reshape(per, TQ, WIN * TQ) + bias[...][None]
        top = jnp.max(s, axis=-1, keepdims=True)
        p = jnp.exp2(s - top)
        total = jnp.sum(p, axis=-1, keepdims=True)
        pb = p.astype(jnp.bfloat16).reshape(per * TQ, WIN * TQ)
        o = jnp.dot(pb, v, preferred_element_type=jnp.float32).reshape(per, TQ, HD)
        o = (o / total).astype(jnp.bfloat16)
        for e in range(per):
            at = pl.ds(pl.multiple_of((i * per + e) * HD, HD), HD)
            out_ref[:, at] = o[e]
            racc[...] += o[e].astype(jnp.float32) * rw_ref[:, at]
        return carry

    lax.fori_loop(0, HQ // 2, heads, 0)

    lane_row = lane[:1]
    following = jnp.where(
        lane_row == TQ - 1, pltpu.roll(segbuf[(ctx + 1) % 16], TQ - 1, 1), pltpu.roll(seg_row, TQ - 1, 1)
    )
    last = (lane_row == TQ - 1) & (ctx == 15)
    is_end = jnp.where((following != seg_row) | last, 1.0, 0.0)
    bin_row = jnp.zeros((1, TQ), jnp.int32)
    for s in range(SEGS):
        bin_row = jnp.where(seg_row == s, bins_ref[0, s], bin_row)
    end_col = column(is_end)
    bin_col = column(bin_row)
    reward = jnp.sum(racc[...], axis=1, keepdims=True)
    kept = jnp.where(end_col > 0.5, reward, 0.0)
    parts = []
    for k in range(BINS // TQ):
        hit = bin_col == (lane + k * TQ).astype(jnp.float32)
        parts.append(jnp.sum(jnp.where(hit, kept, 0.0), axis=0, keepdims=True))
    hist_a[dp] = jnp.concatenate(parts, axis=1)

    def hist_copy(buf, ss, rs, axis, me, k):
        return remote(buf.at[me], buf.at[me], ss.at[k], rs.at[me], {axis: (me + k) % 16})

    def hist_round(buf, ss, rs, axis, me):
        def start(k, carry):
            hist_copy(buf, ss, rs, axis, me, k).start()
            return carry

        def wait(k, carry):
            s = (me + k) % 16
            remote(buf.at[s], buf.at[s], ss.at[k], rs.at[s], {axis: s}).wait_recv()
            return carry

        lax.fori_loop(1, 16, start, 0)
        lax.fori_loop(1, 16, wait, 0)
        return jnp.sum(buf[...], axis=0)

    hist_b[ctx] = hist_round(hist_a, ha_ss, ha_rs, "dp", dp)
    hist_ref[...] = hist_round(hist_b, hb_ss, hb_rs, "ctx", ctx)

    def drain(k, carry):
        kv_copy(k).wait_send()
        q_copy(k).wait_send()
        seg_copy(k).wait_send()
        hist_copy(hist_a, ha_ss, ha_rs, "dp", dp, k).wait_send()
        hist_copy(hist_b, hb_ss, hb_rs, "ctx", ctx, k).wait_send()
        return carry

    lax.fori_loop(1, 16, drain, 0)
    sends = jnp.int32(0)
    for c, steps in enumerate(ROUTES):
        sends += jnp.where(ctx == c, sum(n >= 0 for n in steps), 0)

    def drain_items(slot, carry):
        item_copy(0, 0, ctx, slot).wait_send()
        return carry

    lax.fori_loop(0, sends, drain_items, 0)


def local(roll_query, roll_keys, roll_values, pack_dest, segment_ids, reward_bins, reward_weight):
    vmem = pl.BlockSpec(memory_space=pltpu.VMEM)
    smem = pl.BlockSpec(memory_space=pltpu.SMEM)
    bf16, f32, i32 = jnp.bfloat16, jnp.float32, jnp.int32
    dma = pltpu.SemaphoreType.DMA
    most = max(sum(n >= 0 for n in steps) for steps in ROUTES)
    out, hist = pl.pallas_call(
        kernel,
        out_shape=(jax.ShapeDtypeStruct((TQ, HQ * HD), bf16), jax.ShapeDtypeStruct((1, BINS), f32)),
        in_specs=[smem, smem, vmem, vmem, vmem, vmem, vmem],
        out_specs=(vmem, vmem),
        scratch_shapes=[
            pltpu.VMEM((16, BLK, HQ * HD), bf16),
            pltpu.VMEM((16, BLK, HQ * HD), bf16),
            pltpu.VMEM((16, BLK, 2 * HK * HD), bf16),
            pltpu.VMEM((16, BLK, 2 * HK * HD), bf16),
            pltpu.VMEM((HQ, TQ, HD), bf16),
            pltpu.VMEM((2, 16, HK, TQ, HD), bf16),
            pltpu.VMEM((16, 1, TQ), i32),
            pltpu.VMEM((TQ, WIN * TQ), f32),
            pltpu.VMEM((TQ, HD), f32),
            pltpu.VMEM((16, 1, BINS), f32),
            pltpu.VMEM((16, 1, BINS), f32),
            dma((16,)), dma((16,)), dma((16,)), dma((16,)), dma((16,)), dma((16,)),
            dma((most,)), dma((32,)), dma((16,)), dma((16,)), dma((16,)), dma((16,)),
        ],
        compiler_params=pltpu.CompilerParams(
            collective_id=0, has_side_effects=True, vmem_limit_bytes=48 * 1024 * 1024
        ),
    )(
        pack_dest,
        reward_bins,
        roll_query.reshape(NB, BLK, HQ * HD),
        roll_keys.reshape(NB, BLK, HK * HD),
        roll_values.reshape(NB, BLK, HK * HD),
        segment_ids.reshape(1, 1, TQ),
        reward_weight.reshape(1, HQ * HD),
    )
    return out.reshape(1, TQ, HQ * HD), hist.reshape(BINS)


def solution(mesh):
    in_specs = (
        P("dp", "ctx", None),
        P("dp", "ctx", None),
        P("dp", "ctx", None),
        P(None, "ctx"),
        P("dp", "ctx"),
        P("dp", None),
        P(),
    )
    out_specs = (P("dp", "ctx", None), P())
    return jax.shard_map(local, mesh=mesh, in_specs=in_specs, out_specs=out_specs, check_vma=False)
```

time: 379 us -> 90.3 us (0.24)
  the two profiles are of different devices: /device:TPU:24 before, /device:TPU:1 now
where the time goes in v1:
time: 90.3 us; the launch traced here: 90 us
  Pallas kernels  83.4 us (92%)
  local copies, waits for them, and re-layouts  5.98 us (7%)
    pallas_call x1, Pallas kernels, local(): pl.pallas_call(kernel, out_shape=(jax.ShapeDtypeStruct((TQ, HQ * HD), bf1...  83.4 us
    unnamed x16, local copies, waits for them, and re-layouts  5.98 us

profile of v1, /device:TPU:1, one launch (start us, length us, event | category | flops | bytes accessed | tf_op | source)
XLA Modules:
  0.0 90.0 jit_solution(8998090036609953228)
XLA Ops:
  0.6 0.0 copy-start.4
  0.6 0.0 copy-start.5
  0.7 0.0 copy-start.6
  0.7 0.7 copy-done.4
  1.3 0.0 copy-done.5
  1.3 0.0 copy-done.6
  1.3 0.0 copy-start
  1.3 1.2 %copy-done = bf16[1,128,4096]{2,1,0:T(8,128)(2,1)S(1)} copy-done((bf16[1,128,4096]{2,1,0:T(8,128)(2,1)S(1)}, bf16[1,128,4096]{2,1,0:T(8,128)(2,1)}, u32[]{:S(2)}) %copy-start) | copy-done | bytes 1048600
  2.6 0.0 copy-start.1
  2.6 0.9 %copy-done.1 = bf16[1,128,512]{2,1,0:T(8,128)(2,1)S(1)} copy-done((bf16[1,128,512]{2,1,0:T(8,128)(2,1)S(1)}, bf16[1,128,512]{2,1,0:T(8,128)(2,1)}, u32[]{:S(2)}) %copy-start.1) | copy-done | bytes 131096
  3.5 0.0 copy-start.2
  3.5 0.9 %copy-done.2 = bf16[1,128,512]{2,1,0:T(8,128)(2,1)S(1)} copy-done((bf16[1,128,512]{2,1,0:T(8,128)(2,1)S(1)}, bf16[1,128,512]{2,1,0:T(8,128)(2,1)}, u32[]{:S(2)}) %copy-start.2) | copy-done | bytes 131096
  4.4 0.0 copy-start.3
  4.4 0.7 copy-done.3
  5.1 83.4 %shard_map.86 = (bf16[128,4096]{1,0:T(8,128)(2,1)S(1)}, f32[1,512]{1,0:T(1,128)S(1)}) custom-call(s32[16,16]{1,0:T(8,128)S(1)} %copy-done.4, s32[1,16]{1,0:T(1,128)S(1)} %copy-done.5, bf16[16,8,4096]{2,1,0:T(8,128)(2,1)S(1)} %bitcast.7, bf16[16,8,512]{2,1,0:T(8,128)(2,1)S(1)} %bitcast.9, bf16[16,8,512]{2,1,0:T(8,128)(2,1)S(1)} %bitcast.10, ...), custom_call_target="tpu_custom_call" | custom-call | tf_op jit(solution)/shard_map/pallas_call | solution.py:303
  88.5 1.0 %copy.11 = bf16[1,128,4096]{2,1,0:T(8,128)(2,1)} copy(bf16[1,128,4096]{2,1,0:T(8,128)(2,1)S(1)} %bitcast.8) | data formatting | bytes 2097152
  89.5 0.6 copy.12
Async XLA Ops:
  0.6 0.7 copy-start.4
  0.6 0.7 copy-start.5
  0.7 0.7 copy-start.6
  1.3 1.2 %copy-start = (bf16[1,128,4096]{2,1,0:T(8,128)(2,1)S(1)}, bf16[1,128,4096]{2,1,0:T(8,128)(2,1)}, u32[]{:S(2)}) copy-start(bf16[1,128,4096]{2,1,0:T(8,128)(2,1)} %param.7) | copy-start | bytes 3145732
  2.6 0.9 %copy-start.1 = (bf16[1,128,512]{2,1,0:T(8,128)(2,1)S(1)}, bf16[1,128,512]{2,1,0:T(8,128)(2,1)}, u32[]{:S(2)}) copy-start(bf16[1,128,512]{2,1,0:T(8,128)(2,1)} %param.8) | copy-start | bytes 393220
  3.5 0.9 %copy-start.2 = (bf16[1,128,512]{2,1,0:T(8,128)(2,1)S(1)}, bf16[1,128,512]{2,1,0:T(8,128)(2,1)}, u32[]{:S(2)}) copy-start(bf16[1,128,512]{2,1,0:T(8,128)(2,1)} %param.9) | copy-start | bytes 393220
  4.4 0.7 copy-start.3

commit v2 on v1

--- a/solution.py
+++ b/solution.py
@@ -18,28 +18,31 @@
 BINS = 512
 GROUP = HQ // HK
 WIN = 9
+PER = 2
+HALF = 8
 NEG = -1e30
 SCALE = math.log2(math.e) / math.sqrt(HD)
 MESH = pl.DeviceIdType.MESH
 
 ROUTES = (
-    (264, 7, 1, 263, 8, 257, -2, 24, 23, -18, 279, -23, 360, -6, 88, -3, 39, -22, 344),
-    (16, 274, 281, 18, 25, -1, 272, 2, -17, -20, 258, 313, -3, 32),
-    (42, 291, 298, 35, -18, -20, 305, 275, -2, 33, 19, -1, 3, -17, 259),
-    (315, 52, 306, 308, 59, -21, -19, 331, 292, -3, 36, -18, 276, -2, 20, -1, -17),
-    (323, 76, 69, 332, 325, -4, 53, -20, -23, 364, 309, -19, 293, -3, 37, -18, -1, -2, -17),
-    (86, 349, 93, 342, -23, -5, 356, 70, 365, -21, -24, 326, 381, -4, 54, -1, -20, 4, 310, -19, -17, 260, 294, -3, -2, 38, -18),
-    (357, 110, 359, 103, 366, -24, -6, 373, 382, 87, -22, -1, 5, 343, -5, -17, 261, 71, -21, -2, 21, 327, -4, -18, 55, 277, -20, 311, -19, 295, -3),
-    (374, 127, 383, -1, -23, 6, 352, -17, -7, 262, 111, -6, -2, 22, 80, -22, -18, 278, 336, -5, 79, -21, -4, -3, -20, -19),
-    (399, 393, 143, 137, -10, -17, 159, -26, -1, 415, -18, -8, 121, -2, -24, -11, 175, 377, -23, -3, 361, -7, -20, 105, -6, -19, 89, -22, -4, -5, -21),
-    (154, 152, 410, 408, -25, -18, -11, 280, 394, -9, -2, 138, 168, -3, 40, -19, -20, -8, 312, 122, -24, 378, 296, -4, -23, 56, 362, -21, -7, 328, -5, -6, -22),
-    (427, 169, 171, -10, -3, 41, 155, -26, -19, 297, 411, -20, -25, 395, -9, -4, 57, 139, -21, 329, -5, -8, 123, 73, -24, -22, 345, -23, -7, -6),
-    (188, 444, -27, -20, 314, 428, -11, -4, 172, 58, -10, -5, -21, 330, 156, -26, -22, 412, 74, -25, -6, 346, 396, -9, -7, 140, 106, -23, -8, 90, -24),
-    (205, 461, -12, -5, 189, 75, -28, -21, 445, -22, -27, 347, 429, -11, -6, 91, -23, 173, -7, -10, 107, -26, -24, 363, -8, -25, 379, -9),
-    (222, 478, -13, -22, 206, 348, -29, -6, 462, 92, -7, -12, -23, 190, 108, -28, -25, -24, 380, 446, -8, -27, 124, 430, -10, -11, -26, -9),
-    (239, 495, -14, -7, 223, 109, -30, -23, -25, 479, 397, -13, -24, -8, 125, 207, -29, -10, 157, 463, -12, -26, 191, 413, -28, -9, 141, 447, -27, -11, 431),
-    (-25, -15, 398, -8, 120, -31, -9, 126, -24, 376, -14, -10, 158, -30, -26, 414, -7, 104, -13, 142, -11, -29, 174, -5, -12, 72, -28, -27),
+    (264, 7, 1, 263, 257, -18, 8, 279, -2, -7, 104, 23, -19, 295, -3, 24, -22, 39, 337, -20, 344, 311, 312),
+    (272, 281, 18, 16, 274, -1, -19, 297, 288, 2, -17, -3, 32, 25, 258, -20, 304, 313, -22, 345),
+    (35, 42, 289, 291, 33, -20, -2, 314, 19, 305, -18, -21, 275, 330, -1, 3, -6, -17, 90, 259, -7, 106),
+    (306, 52, 59, 308, -21, -3, 322, 331, 36, -19, -6, 82, 292, 91, -2, 20, -7, -18, 98, 107, 276, -1, 315, -17),
+    (323, 76, 325, 69, -4, -6, 83, 92, 53, -20, -7, 99, 108, 309, -3, 37, -19, -24, 380, 293, -2, -1, 332, -18, -17),
+    (84, 349, 342, 86, -7, -21, 100, 109, 326, -5, -24, 372, 381, 70, -4, 54, -1, -20, 4, 93, 310, -17, -3, 260, 38, -18, -19, -2),
+    (101, 366, 103, 359, -24, -22, 373, 382, 343, -6, -1, 5, 110, 87, -21, -17, 261, 327, -5, -18, 277, 71, -4, -2, 21, 55, -20, -19, -3),
+    (374, 127, -1, -7, 6, 96, 383, -17, -23, 262, 367, -18, -22, 278, 336, -2, -6, 22, 95, -19, -21, 294, -3, -5, -20, -4),
+    (393, 143, 137, 399, -10, 159, -17, -26, 415, -11, -1, -8, 121, 175, -18, -7, -24, -19, 377, -3, 105, -2, -23, -4, 361, -22, -6, -21, -5, -20),
+    (410, 152, 154, 408, -25, -11, 394, 168, -18, -9, 138, 280, -19, -3, 298, 296, 40, -2, -8, -4, 122, 56, -20, -24, -21, 378, 328, -7, -5, 72, -22, -23, -6),
+    (169, 427, 171, -26, 411, -3, -10, 41, 155, -25, -20, -4, 57, 395, -9, 139, -21, -19, -5, 329, 73, -6, -8, -22, 123, 89, -7, -24, -23),
+    (444, 188, -27, 428, -4, -11, 58, 172, -26, -21, -5, 412, 74, -10, 156, -6, -22, -25, 346, 396, -9, -7, -23, 362, -20, -24, -8),
+    (205, 461, -28, 445, -5, -12, 75, 189, -27, -6, -22, 347, 429, -11, 173, -7, -23, -26, 363, 413, -9, -10, -24, 379, -8, -25, -21),
+    (222, 478, -13, 206, -22, -29, 348, 462, -28, -7, -23, 446, 364, -12, -9, 190, 140, -24, -27, -8, 430, 124, -11, -6, -10, -26, -25),
+    (239, 495, -14, 223, -23, -30, 365, -9, 479, -13, 141, -24, -8, 207, -29, 125, -10, 463, -7, -28, 157, -25, 447, -12, 397, -11, 191, -27, -26, 431),
+    (-9, -15, 142, -8, -25, -31, 120, 126, -10, -14, 158, -24, 376, -26, -30, 398, -23, -11, -13, 360, 174, -29, 414, -6, 88, -28, -12, -27),
 )
+CUTS = (22, 20, 22, 24, 25, 28, 29, 26, 24, 27, 25, 24, 26, 26, 28, 26)
 
 
 def remote(src, dst, send_sem, recv_sem, device_id):
@@ -49,19 +52,21 @@
 
 
 def kernel(
-    dest_ref, bins_ref, rq_ref, rk_ref, rv_ref, seg_ref, rw_ref,
+    dest_ref, bins_ref, rq_hbm, rk_hbm, rv_hbm, seg_ref, rw_hbm,
     out_ref, hist_ref,
-    qsend, qrecv, kvsend, kvrecv, qs, kv, segbuf, bias, racc, hist_a, hist_b,
-    q_ss, q_rs, kv_ss, kv_rs, seg_ss, seg_rs, item_ss, item_rs, ha_ss, ha_rs, hb_ss, hb_rs,
+    rq_ref, rk_ref, rv_ref, rw_ref, qsend, qrecv, kvsend, kvrecv, qs, qe, kv, segbuf, bias, bias_end, hist_a, hist_b,
+    in_sem, q_ss, q_rs, kv_ss, kv_rs, seg_ss, seg_rs, item_ss, item_rs, ha_ss, ha_rs, hb_ss, hb_rs,
 ):
     dp = lax.axis_index("dp")
     ctx = lax.axis_index("ctx")
-
-    for b in range(1, WIN):
-        @pl.when(b > ctx)
-        def _():
-            for h in range(2):
-                kv[h, b] = jnp.zeros((HK, TQ, HD), jnp.bfloat16)
+    loads = [
+        pltpu.make_async_copy(src, dst, in_sem.at[i])
+        for i, (src, dst) in enumerate(
+            ((rk_hbm, rk_ref), (rv_hbm, rv_ref), (rq_hbm, rq_ref), (rw_hbm, rw_ref))
+        )
+    ]
+    for load in loads:
+        load.start()
 
     barrier = pltpu.get_barrier_semaphore()
 
@@ -80,6 +85,8 @@
         kvsend[d, :, HK * HD :] = rv_ref[inv]
         return carry
 
+    loads[0].wait()
+    loads[1].wait()
     lax.fori_loop(0, NB, fill_kv, 0)
     pl.semaphore_wait(barrier, 30)
 
@@ -109,7 +116,9 @@
         qsend[d] = rq_ref[inv]
         return carry
 
+    loads[2].wait()
     lax.fori_loop(0, NB, fill_q, 0)
+    loads[3].wait()
 
     def q_copy(k):
         d = (dp + k) % 16
@@ -160,6 +169,7 @@
         return slot
 
     first = [next((i for i, n in enumerate(steps) if n < 0), len(steps)) for steps in ROUTES]
+    sent = [sum(n >= 0 for n in steps[:cut]) for steps, cut in zip(ROUTES, CUTS)]
     for c, steps in enumerate(ROUTES):
         @pl.when(ctx == c)
         def _():
@@ -171,7 +181,11 @@
     for c, steps in enumerate(ROUTES):
         @pl.when(ctx == c)
         def _():
-            run_steps(steps[first[c] :], first[c])
+            for h in range(2):
+                for b in range(c + 1, WIN):
+                    if -1 - (h * 16 + b) not in steps:
+                        kv[h, b] = jnp.zeros((HK, TQ, HD), jnp.bfloat16)
+            run_steps(steps[first[c] : CUTS[c]], first[c])
 
     def q_wait(k, carry):
         s = (dp + k) % 16
@@ -211,68 +225,90 @@
         allowed = (seg_col == keys) & ((base + w - ctx) * TQ + lane <= sub)
         bias[:, w * TQ : (w + 1) * TQ] = jnp.where(allowed, 0.0, NEG)
 
-    racc[...] = jnp.zeros_like(racc)
-
-    def heads(i, carry):
-        per = 2
-        g = i // (GROUP // per)
-        q = qs[pl.ds(i * per, per)].reshape(per * TQ, HD)
+    wide = (SEGS, TQ)
+    lane_row = lane[:1]
+    end_lane = lax.broadcasted_iota(jnp.int32, wide, 1).astype(jnp.float32)
+    end_seg = lax.broadcasted_iota(jnp.int32, wide, 0)
+    following = jnp.where(
+        lane_row == TQ - 1, pltpu.roll(segbuf[(ctx + 1) % 16], TQ - 1, 1), pltpu.roll(seg_row, TQ - 1, 1)
+    )
+    is_end = (following != seg_row) | ((lane_row == TQ - 1) & (ctx == 15))
+    pick = jnp.where((seg_row == end_seg) & is_end, 1.0, 0.0)
+    end_pos = jnp.sum(pick * end_lane, axis=1, keepdims=True)
+    has_end = jnp.sum(pick, axis=1, keepdims=True)
+    pick = pick.astype(jnp.bfloat16)
+    for w in range(WIN):
+        offset = ((base + w - ctx) * TQ).astype(jnp.float32)
+        allowed = (segbuf[base + w] == end_seg) & (end_lane + offset <= end_pos)
+        bias_end[:, w * TQ : (w + 1) * TQ] = jnp.where(allowed, 0.0, NEG)
+    for h in range(HQ):
+        rows = jnp.dot(pick, qs[h], preferred_element_type=jnp.float32).astype(jnp.bfloat16)
+        qe[h // GROUP, (h % GROUP) * SEGS : (h % GROUP + 1) * SEGS] = rows
+
+    for c, steps in enumerate(ROUTES):
+        @pl.when(ctx == c)
+        def _():
+            run_steps(steps[CUTS[c] :], sent[c])
+
+    def attend(q, g, mask, per, rows):
         k = kv[0, pl.ds(base, WIN), g].reshape(WIN * TQ, HD)
         v = kv[1, pl.ds(base, WIN), g].reshape(WIN * TQ, HD)
         s = lax.dot_general(q, k, (((1,), (1,)), ((), ())), preferred_element_type=jnp.float32)
-        s = (s * SCALE).reshape(per, TQ, WIN * TQ) + bias[...][None]
+        s = (s * SCALE).reshape(per, rows, WIN * TQ) + mask[None]
         top = jnp.max(s, axis=-1, keepdims=True)
         p = jnp.exp2(s - top)
         total = jnp.sum(p, axis=-1, keepdims=True)
-        pb = p.astype(jnp.bfloat16).reshape(per * TQ, WIN * TQ)
-        o = jnp.dot(pb, v, preferred_element_type=jnp.float32).reshape(per, TQ, HD)
-        o = (o / total).astype(jnp.bfloat16)
+        pb = p.astype(jnp.bfloat16).reshape(per * rows, WIN * TQ)
+        o = jnp.dot(pb, v, preferred_element_type=jnp.float32).reshape(per, rows, HD)
+        return (o / total).astype(jnp.bfloat16)
+
+    terms = jnp.zeros((SEGS, HD), jnp.float32)
+    for g in range(HK):
+        o = attend(qe[g], g, bias_end[...], GROUP, SEGS)
+        for j in range(GROUP):
+            h = g * GROUP + j
+            terms += o[j].astype(jnp.float32) * rw_ref[h : h + 1, :]
+    reward = jnp.where(has_end > 0.5, jnp.sum(terms, axis=1, keepdims=True), 0.0)
+    bin_seg = lax.broadcasted_iota(jnp.int32, (SEGS, BINS), 0)
+    bin_lane = lax.broadcasted_iota(jnp.int32, (SEGS, BINS), 1)
+    bin_of = jnp.zeros((SEGS, BINS), jnp.int32)
+    for s in range(SEGS):
+        bin_of = jnp.where(bin_seg == s, bins_ref[0, s], bin_of)
+    hist_a[dp] = jnp.sum(jnp.where(bin_of == bin_lane, reward, 0.0), axis=0, keepdims=True)
+
+    def heads(i, carry):
+        per = PER
+        o = attend(qs[pl.ds(i * per, per)].reshape(per * TQ, HD), i // (GROUP // per), bias[...], per, TQ)
         for e in range(per):
             at = pl.ds(pl.multiple_of((i * per + e) * HD, HD), HD)
             out_ref[:, at] = o[e]
-            racc[...] += o[e].astype(jnp.float32) * rw_ref[:, at]
-        return carry
-
-    lax.fori_loop(0, HQ // 2, heads, 0)
-
-    lane_row = lane[:1]
-    following = jnp.where(
-        lane_row == TQ - 1, pltpu.roll(segbuf[(ctx + 1) % 16], TQ - 1, 1), pltpu.roll(seg_row, TQ - 1, 1)
-    )
-    last = (lane_row == TQ - 1) & (ctx == 15)
-    is_end = jnp.where((following != seg_row) | last, 1.0, 0.0)
-    bin_row = jnp.zeros((1, TQ), jnp.int32)
-    for s in range(SEGS):
-        bin_row = jnp.where(seg_row == s, bins_ref[0, s], bin_row)
-    end_col = column(is_end)
-    bin_col = column(bin_row)
-    reward = jnp.sum(racc[...], axis=1, keepdims=True)
-    kept = jnp.where(end_col > 0.5, reward, 0.0)
-    parts = []
-    for k in range(BINS // TQ):
-        hit = bin_col == (lane + k * TQ).astype(jnp.float32)
-        parts.append(jnp.sum(jnp.where(hit, kept, 0.0), axis=0, keepdims=True))
-    hist_a[dp] = jnp.concatenate(parts, axis=1)
+        return carry
 
     def hist_copy(buf, ss, rs, axis, me, k):
         return remote(buf.at[me], buf.at[me], ss.at[k], rs.at[me], {axis: (me + k) % 16})
 
-    def hist_round(buf, ss, rs, axis, me):
+    def hist_start(buf, ss, rs, axis, me):
         def start(k, carry):
             hist_copy(buf, ss, rs, axis, me, k).start()
             return carry
 
+        lax.fori_loop(1, 16, start, 0)
+
+    def hist_total(buf, ss, rs, axis, me):
         def wait(k, carry):
             s = (me + k) % 16
             remote(buf.at[s], buf.at[s], ss.at[k], rs.at[s], {axis: s}).wait_recv()
             return carry
 
-        lax.fori_loop(1, 16, start, 0)
         lax.fori_loop(1, 16, wait, 0)
         return jnp.sum(buf[...], axis=0)
 
-    hist_b[ctx] = hist_round(hist_a, ha_ss, ha_rs, "dp", dp)
-    hist_ref[...] = hist_round(hist_b, hb_ss, hb_rs, "ctx", ctx)
+    hist_start(hist_a, ha_ss, ha_rs, "dp", dp)
+    lax.fori_loop(0, HALF, heads, 0)
+    hist_b[ctx] = hist_total(hist_a, ha_ss, ha_rs, "dp", dp)
+    hist_start(hist_b, hb_ss, hb_rs, "ctx", ctx)
+    lax.fori_loop(HALF, HQ // PER, heads, 0)
+    hist_ref[...] = hist_total(hist_b, hb_ss, hb_rs, "ctx", ctx)
 
     def drain(k, carry):
         kv_copy(k).wait_send()
@@ -297,31 +333,37 @@
 def local(roll_query, roll_keys, roll_values, pack_dest, segment_ids, reward_bins, reward_weight):
     vmem = pl.BlockSpec(memory_space=pltpu.VMEM)
     smem = pl.BlockSpec(memory_space=pltpu.SMEM)
+    hbm = pl.BlockSpec(memory_space=pltpu.HBM)
     bf16, f32, i32 = jnp.bfloat16, jnp.float32, jnp.int32
     dma = pltpu.SemaphoreType.DMA
     most = max(sum(n >= 0 for n in steps) for steps in ROUTES)
     out, hist = pl.pallas_call(
         kernel,
         out_shape=(jax.ShapeDtypeStruct((TQ, HQ * HD), bf16), jax.ShapeDtypeStruct((1, BINS), f32)),
-        in_specs=[smem, smem, vmem, vmem, vmem, vmem, vmem],
+        in_specs=[smem, smem, hbm, hbm, hbm, vmem, hbm],
         out_specs=(vmem, vmem),
         scratch_shapes=[
+            pltpu.VMEM((NB, BLK, HQ * HD), bf16),
+            pltpu.VMEM((NB, BLK, HK * HD), bf16),
+            pltpu.VMEM((NB, BLK, HK * HD), bf16),
+            pltpu.VMEM((HQ, HD), f32),
             pltpu.VMEM((16, BLK, HQ * HD), bf16),
             pltpu.VMEM((16, BLK, HQ * HD), bf16),
             pltpu.VMEM((16, BLK, 2 * HK * HD), bf16),
             pltpu.VMEM((16, BLK, 2 * HK * HD), bf16),
             pltpu.VMEM((HQ, TQ, HD), bf16),
+            pltpu.VMEM((HK, GROUP * SEGS, HD), bf16),
             pltpu.VMEM((2, 16, HK, TQ, HD), bf16),
             pltpu.VMEM((16, 1, TQ), i32),
             pltpu.VMEM((TQ, WIN * TQ), f32),
-            pltpu.VMEM((TQ, HD), f32),
+            pltpu.VMEM((SEGS, WIN * TQ), f32),
             pltpu.VMEM((16, 1, BINS), f32),
             pltpu.VMEM((16, 1, BINS), f32),
-            dma((16,)), dma((16,)), dma((16,)), dma((16,)), dma((16,)), dma((16,)),
+            dma((4,)), dma((16,)), dma((16,)), dma((16,)), dma((16,)), dma((16,)), dma((16,)),
             dma((most,)), dma((32,)), dma((16,)), dma((16,)), dma((16,)), dma((16,)),
         ],
         compiler_params=pltpu.CompilerParams(
-            collective_id=0, has_side_effects=True, vmem_limit_bytes=48 * 1024 * 1024
+            collective_id=0, has_side_effects=True, vmem_limit_bytes=60 * 1024 * 1024
         ),
     )(
         pack_dest,
@@ -330,7 +372,7 @@
         roll_keys.reshape(NB, BLK, HK * HD),
         roll_values.reshape(NB, BLK, HK * HD),
         segment_ids.reshape(1, 1, TQ),
-        reward_weight.reshape(1, HQ * HD),
+        reward_weight.reshape(HQ, HD),
     )
     return out.reshape(1, TQ, HQ * HD), hist.reshape(BINS)
 

time: 90.3 us -> 76 us (0.84)
  the two profiles are of different devices: /device:TPU:1 before, /device:TPU:24 now
where the time goes in v2:
time: 76 us; the launch traced here: 75.8 us
  Pallas kernels  72.3 us (95%)
  local copies, waits for them, and re-layouts  2.87 us (4%)
    pallas_call x1, Pallas kernels, local(): pl.pallas_call(kernel, out_shape=(jax.ShapeDtypeStruct((TQ, HQ * HD), bf1...  72.3 us
    unnamed x4, local copies, waits for them, and re-layouts  2.87 us

profile of v2, /device:TPU:24, one launch (start us, length us, event | category | flops | bytes accessed | tf_op | source)
XLA Modules:
  0.0 75.8 jit_solution(7940870833981065255)
XLA Ops:
  0.6 72.3 %shard_map.86 = (bf16[128,4096]{1,0:T(8,128)(2,1)}, f32[1,512]{1,0:T(1,128)}) custom-call(s32[16,16]{1,0:T(8,128)} %dest_ref.1, s32[1,16]{1,0:T(1,128)} %bins_ref.1, bf16[16,8,4096]{2,1,0:T(8,128)(2,1)} %bitcast.7, bf16[16,8,512]{2,1,0:T(8,128)(2,1)} %bitcast.9, bf16[16,8,512]{2,1,0:T(8,128)(2,1)} %bitcast.10, s32[1,1,128]{2,1,0:T(1,128)} %bitcast.13, ...), custom_call_target="tpu_custom_call" | custom-call | tf_op jit(solution)/shard_map/pallas_call | solution.py:340
  73.0 0.0 copy-start
  73.0 2.3 %copy.11 = bf16[1,128,4096]{2,1,0:T(8,128)(2,1)} copy(bf16[1,128,4096]{2,1,0:T(8,128)(2,1)} %bitcast.8) | data formatting | bytes 2097152
  75.3 0.0 copy-done
  75.3 0.6 copy.12
Async XLA Ops:
  73.0 2.3 %copy-start = (f32[1,512]{1,0:T(1,128)S(1)}, f32[1,512]{1,0:T(1,128)}, u32[]{:S(2)}) copy-start(f32[1,512]{1,0:T(1,128)} %get-tuple-element.5) | copy-start | bytes 6148

commit v3 on v2

v3 whole, which is shorter than its diff:
```python
import functools
import math

import jax
import jax.numpy as jnp
from jax import lax
from jax.experimental import pallas as pl
from jax.experimental.pallas import tpu as pltpu
from jax.sharding import PartitionSpec as P

HQ = 32
HK = 4
HD = 128
TQ = 128
BLK = 8
NB = 16
SEGS = 16
BINS = 512
GROUP = HQ // HK
WIN = 9
PER = 2
HALF = 8
NEG = -1e30
SCALE = math.log2(math.e) / math.sqrt(HD)
MESH = pl.DeviceIdType.MESH

ROUTES = (
    (264, 7, 1, 263, 257, -18, 8, 279, -2, -7, 104, 23, -19, 295, -3, 24, -22, 39, 337, -20, 344, 311, 312),
    (272, 281, 18, 16, 274, -1, -19, 297, 288, 2, -17, -3, 32, 25, 258, -20, 304, 313, -22, 345),
    (35, 42, 289, 291, 33, -20, -2, 314, 19, 305, -18, -21, 275, 330, -1, 3, -6, -17, 90, 259, -7, 106),
    (306, 52, 59, 308, -21, -3, 322, 331, 36, -19, -6, 82, 292, 91, -2, 20, -7, -18, 98, 107, 276, -1, 315, -17),
    (323, 76, 325, 69, -4, -6, 83, 92, 53, -20, -7, 99, 108, 309, -3, 37, -19, -24, 380, 293, -2, -1, 332, -18, -17),
    (84, 349, 342, 86, -7, -21, 100, 109, 326, -5, -24, 372, 381, 70, -4, 54, -1, -20, 4, 93, 310, -17, -3, 260, 38, -18, -19, -2),
    (101, 366, 103, 359, -24, -22, 373, 382, 343, -6, -1, 5, 110, 87, -21, -17, 261, 327, -5, -18, 277, 71, -4, -2, 21, 55, -20, -19, -3),
    (374, 127, -1, -7, 6, 96, 383, -17, -23, 262, 367, -18, -22, 278, 336, -2, -6, 22, 95, -19, -21, 294, -3, -5, -20, -4),
    (393, 143, 137, 399, -10, 159, -17, -26, 415, -11, -1, -8, 121, 175, -18, -7, -24, -19, 377, -3, 105, -2, -23, -4, 361, -22, -6, -21, -5, -20),
    (410, 152, 154, 408, -25, -11, 394, 168, -18, -9, 138, 280, -19, -3, 298, 296, 40, -2, -8, -4, 122, 56, -20, -24, -21, 378, 328, -7, -5, 72, -22, -23, -6),
    (169, 427, 171, -26, 411, -3, -10, 41, 155, -25, -20, -4, 57, 395, -9, 139, -21, -19, -5, 329, 73, -6, -8, -22, 123, 89, -7, -24, -23),
    (444, 188, -27, 428, -4, -11, 58, 172, -26, -21, -5, 412, 74, -10, 156, -6, -22, -25, 346, 396, -9, -7, -23, 362, -20, -24, -8),
    (205, 461, -28, 445, -5, -12, 75, 189, -27, -6, -22, 347, 429, -11, 173, -7, -23, -26, 363, 413, -9, -10, -24, 379, -8, -25, -21),
    (222, 478, -13, 206, -22, -29, 348, 462, -28, -7, -23, 446, 364, -12, -9, 190, 140, -24, -27, -8, 430, 124, -11, -6, -10, -26, -25),
    (239, 495, -14, 223, -23, -30, 365, -9, 479, -13, 141, -24, -8, 207, -29, 125, -10, 463, -7, -28, 157, -25, 447, -12, 397, -11, 191, -27, -26, 431),
    (-9, -15, 142, -8, -25, -31, 120, 126, -10, -14, 158, -24, 376, -26, -30, 398, -23, -11, -13, 360, 174, -29, 414, -6, 88, -28, -12, -27),
)
CUTS = (22, 20, 22, 24, 25, 28, 29, 26, 24, 27, 25, 24, 26, 26, 28, 26)


def remote(src, dst, send_sem, recv_sem, device_id):
    return pltpu.make_async_remote_copy(
        src_ref=src, dst_ref=dst, send_sem=send_sem, recv_sem=recv_sem, device_id=device_id, device_id_type=MESH
    )


def kernel(
    dest_ref, bins_ref, rq_hbm, rk_hbm, rv_hbm, seg_ref, rw_hbm,
    out_hbm, hist_ref,
    rq_ref, rk_ref, rv_ref, rw_ref, qsend, qrecv, ksend, krecv, vsend, vrecv, qs, qe, kbuf, vbuf, out_ref, seg_next,
    bias, bias_end, hist_a, hist_b,
    in_sem, out_sem, q_ss, q_rs, k_ss, k_rs, v_ss, v_rs, seg_ss, seg_rs, item_ss, item_rs,
    ha_ss, ha_rs, hb_ss, hb_rs, known,
):
    dp = lax.axis_index("dp")
    ctx = lax.axis_index("ctx")
    line = ctx // 8 * 8
    near = (line + (ctx + 1) % 8, line + (ctx + 7) % 8, (ctx + 8) % 16)
    loads = [
        pltpu.make_async_copy(src, dst, in_sem.at[i])
        for i, (src, dst) in enumerate(
            ((rk_hbm, rk_ref), (rv_hbm, rv_ref), (rq_hbm, rq_ref), (rw_hbm, rw_ref))
        )
    ]
    barrier = pltpu.get_barrier_semaphore()

    def greet(k, carry):
        pl.semaphore_signal(barrier, inc=1, device_id={"dp": (dp + k) % 16}, device_id_type=MESH)
        return carry

    lax.fori_loop(1, 16, greet, 0)
    for to in near:
        pl.semaphore_signal(barrier, inc=1, device_id={"ctx": to}, device_id_type=MESH)

    @pl.when(ctx == 7)
    def _():
        pl.semaphore_signal(barrier, inc=1, device_id={"ctx": 8}, device_id_type=MESH)

    for load in loads:
        load.start()

    def fill(src, dst):
        def body(d, carry):
            inv = jnp.int32(0)
            for j in range(NB):
                inv = jnp.where(dest_ref[dp, j] == d, j, inv)
            dst[d] = src[inv]
            return carry

        lax.fori_loop(0, NB, body, 0)

    def exchange(send, recv, ss, rs):
        def copy(k):
            d = (dp + k) % 16
            return remote(send.at[d], recv.at[dp], ss.at[k], rs.at[dp], {"dp": d})

        def start(k, carry):
            copy(k).start()
            return carry

        def wait(k, carry):
            s = (dp + k) % 16
            remote(send.at[s], recv.at[s], ss.at[k], rs.at[s], {"dp": s}).wait_recv()
            return carry

        return copy, start, wait

    k_copy, k_start, k_wait = exchange(ksend, krecv, k_ss, k_rs)
    v_copy, v_start, v_wait = exchange(vsend, vrecv, v_ss, v_rs)
    q_copy, q_start, q_wait = exchange(qsend, qrecv, q_ss, q_rs)
    loads[0].wait()
    fill(rk_ref, ksend)
    loads[1].wait()
    fill(rv_ref, vsend)
    pl.semaphore_wait(barrier, 18 + jnp.where(ctx == 8, 1, 0))
    lax.fori_loop(1, 16, k_start, 0)
    lax.fori_loop(1, 16, v_start, 0)
    krecv[dp] = ksend[dp]
    vrecv[dp] = vsend[dp]

    def spread(r):
        for to in near:
            pl.semaphore_signal(known.at[r], inc=1, device_id={"ctx": to}, device_id_type=MESH)

    def heard(r):
        pl.semaphore_wait(known.at[r], 3)

    seg_copy = remote(seg_ref.at[0], seg_next, seg_ss, seg_rs, {"ctx": (ctx + 15) % 16})
    spread(0)

    @pl.when(ctx > 0)
    def _():
        seg_copy.start()

    loads[2].wait()
    fill(rq_ref, qsend)
    loads[3].wait()
    heard(0)
    spread(1)

    def source_of(j):
        src = jnp.int32(0)
        for s in range(16):
            src = jnp.where(dest_ref[s, j] == dp, s, src)
        return src

    def rows_of(recv, jj):
        top = recv[source_of(2 * jj)].astype(jnp.float32)
        low = recv[source_of(2 * jj + 1)].astype(jnp.float32)
        return jnp.concatenate([top, low], axis=0).astype(jnp.bfloat16)

    def pack(recv, buf):
        def body(jj, carry):
            rows = rows_of(recv, jj)
            for g in range(HK):
                at = pl.ds(pl.multiple_of(g * TQ + jj * 16, 16), 16)
                buf[ctx, at, :] = rows[:, g * HD : (g + 1) * HD]
            return carry

        lax.fori_loop(0, NB // 2, body, 0)

    def item_copy(item, to, slot):
        buf = (kbuf, vbuf)[item // 16].at[item % 16]
        return remote(buf, buf, item_ss.at[slot], item_rs.at[item], {"ctx": to})

    slots = []
    for steps in ROUTES:
        k_sends = [n for n in steps if 0 <= n < 256]
        v_sends = [n for n in steps if n >= 256]
        slots.append({n: i for i, n in enumerate(k_sends + v_sends)})

    def run_steps(c, steps):
        for n in steps:
            if n < 0:
                item_copy(-1 - n, ctx, 0).wait_recv()
            else:
                item_copy(n // 16, n % 16, slots[c][n]).start()

    first = [next((i for i, n in enumerate(steps) if n < 0), len(steps)) for steps in ROUTES]
    seg_row = seg_ref[0]
    kbuf[ctx, HK * TQ :, :] = jnp.broadcast_to(seg_row.astype(jnp.float32), (16, TQ)).astype(jnp.bfloat16)
    lax.fori_loop(1, 16, k_wait, 0)
    pack(krecv, kbuf)
    for c, steps in enumerate(ROUTES):
        @pl.when(ctx == c)
        def _():
            run_steps(c, [n for n in steps[: first[c]] if n < 256])

    lax.fori_loop(1, 16, v_wait, 0)
    pack(vrecv, vbuf)
    for c, steps in enumerate(ROUTES):
        @pl.when(ctx == c)
        def _():
            run_steps(c, [n for n in steps[: first[c]] if n >= 256])

    lax.fori_loop(1, 16, q_start, 0)
    qrecv[dp] = qsend[dp]
    heard(1)
    spread(2)
    for c, steps in enumerate(ROUTES):
        @pl.when(ctx == c)
        def _():
            for b in range(c + 1, WIN):
                if -1 - b not in steps:
                    kbuf[b] = jnp.zeros((HK * TQ + 16, HD), jnp.bfloat16)
                if -1 - (16 + b) not in steps:
                    vbuf[b] = jnp.zeros((HK * TQ, HD), jnp.bfloat16)
            run_steps(c, steps[first[c] : CUTS[c]])

    heard(2)
    spread(3)
    lax.fori_loop(1, 16, q_wait, 0)

    def pack_q(jj, carry):
        rows = rows_of(qrecv, jj)
        at = pl.ds(pl.multiple_of(jj * 16, 16), 16)
        for h in range(HQ):
            qs[h, at, :] = rows[:, h * HD : (h + 1) * HD]
        return carry

    lax.fori_loop(0, NB // 2, pack_q, 0)

    @pl.when(ctx < 15)
    def _():
        remote(seg_ref.at[0], seg_next, seg_ss, seg_rs, {"ctx": ctx}).wait_recv()

    def column(row):
        return jnp.transpose(jnp.broadcast_to(row.astype(jnp.float32), (TQ, TQ)))

    lane = lax.broadcasted_iota(jnp.int32, (TQ, TQ), 1)
    sub = lax.broadcasted_iota(jnp.int32, (TQ, TQ), 0)
    seg_col = column(seg_row)
    base = jnp.maximum(ctx - (WIN - 1), 0)
    wide = (SEGS, TQ)
    lane_row = lane[:1]
    end_lane = lax.broadcasted_iota(jnp.int32, wide, 1).astype(jnp.float32)
    end_seg = lax.broadcasted_iota(jnp.int32, wide, 0)
    following = jnp.where(
        lane_row == TQ - 1, pltpu.roll(seg_next[...], TQ - 1, 1), pltpu.roll(seg_row, TQ - 1, 1)
    )
    is_end = (following != seg_row) | ((lane_row == TQ - 1) & (ctx == 15))
    pick = jnp.where((seg_row == end_seg) & is_end, 1.0, 0.0)
    end_pos = jnp.sum(pick * end_lane, axis=1, keepdims=True)
    has_end = jnp.sum(pick, axis=1, keepdims=True)
    pick = pick.astype(jnp.bfloat16)
    for h in range(HQ):
        rows = jnp.dot(pick, qs[h], preferred_element_type=jnp.float32).astype(jnp.bfloat16)
        qe[h // GROUP, (h % GROUP) * SEGS : (h % GROUP + 1) * SEGS] = rows

    for c, steps in enumerate(ROUTES):
        @pl.when(ctx == c)
        def _():
            run_steps(c, steps[CUTS[c] :])

    heard(3)
    end_seg_f = end_seg.astype(jnp.float32)
    for w in range(WIN):
        keys = kbuf[base + w, HK * TQ :, :].astype(jnp.float32)
        offset = (base + w - ctx) * TQ
        at = slice(w * TQ, (w + 1) * TQ)
        ends = (keys == end_seg_f) & (end_lane + offset.astype(jnp.float32) <= end_pos)
        bias_end[:, at] = jnp.where(ends, 0.0, NEG)
        allowed = (seg_col == keys[:1]) & (offset + lane <= sub)
        bias[:, at] = jnp.where(allowed, 0.0, NEG)

    def attend(q, g, mask, per, rows):
        part = pl.ds(pl.multiple_of(g * TQ, TQ), TQ)
        k = kbuf[pl.ds(base, WIN), part, :].reshape(WIN * TQ, HD)
        v = vbuf[pl.ds(base, WIN), part, :].reshape(WIN * TQ, HD)
        s = lax.dot_general(q, k, (((1,), (1,)), ((), ())), preferred_element_type=jnp.float32)
        s = (s * SCALE).reshape(per, rows, WIN * TQ) + mask[None]
        top = jnp.max(s, axis=-1, keepdims=True)
        p = jnp.exp2(s - top)
        total = jnp.sum(p, axis=-1, keepdims=True)
        pb = p.astype(jnp.bfloat16).reshape(per * rows, WIN * TQ)
        o = jnp.dot(pb, v, preferred_element_type=jnp.float32).reshape(per, rows, HD)
        return (o / total).astype(jnp.bfloat16)

    terms = jnp.zeros((SEGS, HD), jnp.float32)
    for g in range(HK):
        o = attend(qe[g], g, bias_end[...], GROUP, SEGS)
        for j in range(GROUP):
            h = g * GROUP + j
            terms += o[j].astype(jnp.float32) * rw_ref[h : h + 1, :]
    reward = jnp.where(has_end > 0.5, jnp.sum(terms, axis=1, keepdims=True), 0.0)
    bin_seg = lax.broadcasted_iota(jnp.int32, (SEGS, BINS), 0)
    bin_lane = lax.broadcasted_iota(jnp.int32, (SEGS, BINS), 1)
    bin_of = jnp.zeros((SEGS, BINS), jnp.int32)
    for s in range(SEGS):
        bin_of = jnp.where(bin_seg == s, bins_ref[0, s], bin_of)
    hist_a[dp] = jnp.sum(jnp.where(bin_of == bin_lane, reward, 0.0), axis=0, keepdims=True)

    def out_copy(i):
        at = pl.ds(pl.multiple_of(i * PER * HD, PER * HD), PER * HD)
        return pltpu.make_async_copy(out_ref.at[:, at], out_hbm.at[:, at], out_sem.at[i])

    def heads(i, carry):
        per = PER
        o = attend(qs[pl.ds(i * per, per)].reshape(per * TQ, HD), i // (GROUP // per), bias[...], per, TQ)
        for e in range(per):
            at = pl.ds(pl.multiple_of((i * per + e) * HD, HD), HD)
            out_ref[:, at] = o[e]
        out_copy(i).start()
        return carry

    def hist_copy(buf, ss, rs, axis, me, k):
        return remote(buf.at[me], buf.at[me], ss.at[k], rs.at[me], {axis: (me + k) % 16})

    def hist_start(buf, ss, rs, axis, me):
        def start(k, carry):
            hist_copy(buf, ss, rs, axis, me, k).start()
            return carry

        lax.fori_loop(1, 16, start, 0)

    def hist_total(buf, ss, rs, axis, me):
        def wait(k, carry):
            s = (me + k) % 16
            remote(buf.at[s], buf.at[s], ss.at[k], rs.at[s], {axis: s}).wait_recv()
            return carry

        lax.fori_loop(1, 16, wait, 0)
        return jnp.sum(buf[...], axis=0)

    hist_start(hist_a, ha_ss, ha_rs, "dp", dp)
    lax.fori_loop(0, HALF, heads, 0)
    hist_b[ctx] = hist_total(hist_a, ha_ss, ha_rs, "dp", dp)
    hist_start(hist_b, hb_ss, hb_rs, "ctx", ctx)
    lax.fori_loop(HALF, HQ // PER, heads, 0)
    hist_ref[...] = hist_total(hist_b, hb_ss, hb_rs, "ctx", ctx)

    def drain(k, carry):
        k_copy(k).wait_send()
        v_copy(k).wait_send()
        q_copy(k).wait_send()
        hist_copy(hist_a, ha_ss, ha_rs, "dp", dp, k).wait_send()
        hist_copy(hist_b, hb_ss, hb_rs, "ctx", ctx, k).wait_send()
        return carry

    lax.fori_loop(1, 16, drain, 0)

    @pl.when(ctx > 0)
    def _():
        seg_copy.wait_send()

    def counted(low, high):
        total = jnp.int32(0)
        for c, steps in enumerate(ROUTES):
            total += jnp.where(ctx == c, sum(low <= n < high for n in steps), 0)
        return total

    k_sends = counted(0, 256)

    def drain_items(item):
        def body(slot, carry):
            item_copy(item, ctx, slot).wait_send()
            return carry

        return body

    lax.fori_loop(0, k_sends, drain_items(0), 0)
    lax.fori_loop(k_sends, k_sends + counted(256, 512), drain_items(16), 0)

    def drain_out(i, carry):
        out_copy(i).wait()
        return carry

    lax.fori_loop(0, HQ // PER, drain_out, 0)


def local(roll_query, roll_keys, roll_values, pack_dest, segment_ids, reward_bins, reward_weight):
    vmem = pl.BlockSpec(memory_space=pltpu.VMEM)
    smem = pl.BlockSpec(memory_space=pltpu.SMEM)
    hbm = pl.BlockSpec(memory_space=pltpu.HBM)
    bf16, f32, i32 = jnp.bfloat16, jnp.float32, jnp.int32
    dma = pltpu.SemaphoreType.DMA
    most = max(sum(n >= 0 for n in steps) for steps in ROUTES)
    out, hist = pl.pallas_call(
        kernel,
        out_shape=(jax.ShapeDtypeStruct((TQ, HQ * HD), bf16), jax.ShapeDtypeStruct((1, BINS), f32)),
        in_specs=[smem, smem, hbm, hbm, hbm, vmem, hbm],
        out_specs=(hbm, vmem),
        scratch_shapes=[
            pltpu.VMEM((NB, BLK, HQ * HD), bf16),
            pltpu.VMEM((NB, BLK, HK * HD), bf16),
            pltpu.VMEM((NB, BLK, HK * HD), bf16),
            pltpu.VMEM((HQ, HD), f32),
            pltpu.VMEM((16, BLK, HQ * HD), bf16),
            pltpu.VMEM((16, BLK, HQ * HD), bf16),
            pltpu.VMEM((16, BLK, HK * HD), bf16),
            pltpu.VMEM((16, BLK, HK * HD), bf16),
            pltpu.VMEM((16, BLK, HK * HD), bf16),
            pltpu.VMEM((16, BLK, HK * HD), bf16),
            pltpu.VMEM((HQ, TQ, HD), bf16),
            pltpu.VMEM((HK, GROUP * SEGS, HD), bf16),
            pltpu.VMEM((16, HK * TQ + 16, HD), bf16),
            pltpu.VMEM((16, HK * TQ, HD), bf16),
            pltpu.VMEM((TQ, HQ * HD), bf16),
            pltpu.VMEM((1, TQ), i32),
            pltpu.VMEM((TQ, WIN * TQ), f32),
            pltpu.VMEM((SEGS, WIN * TQ), f32),
            pltpu.VMEM((16, 1, BINS), f32),
            pltpu.VMEM((16, 1, BINS), f32),
            dma((4,)), dma((HQ // PER,)), dma((16,)), dma((16,)), dma((16,)), dma((16,)), dma((16,)), dma((16,)),
            dma, dma, dma((most,)), dma((32,)), dma((16,)), dma((16,)), dma((16,)), dma((16,)),
            pltpu.SemaphoreType.REGULAR((4,)),
        ],
        compiler_params=pltpu.CompilerParams(
            collective_id=0, has_side_effects=True, vmem_limit_bytes=60 * 1024 * 1024
        ),
    )(
        pack_dest,
        reward_bins,
        roll_query.reshape(NB, BLK, HQ * HD),
        roll_keys.reshape(NB, BLK, HK * HD),
        roll_values.reshape(NB, BLK, HK * HD),
        segment_ids.reshape(1, 1, TQ),
        reward_weight.reshape(HQ, HD),
    )
    return out.reshape(1, TQ, HQ * HD), hist.reshape(BINS)


def solution(mesh):
    in_specs = (
        P("dp", "ctx", None),
        P("dp", "ctx", None),
        P("dp", "ctx", None),
        P(None, "ctx"),
        P("dp", "ctx"),
        P("dp", None),
        P(),
    )
    out_specs = (P("dp", "ctx", None), P())
    return jax.shard_map(local, mesh=mesh, in_specs=in_specs, out_specs=out_specs, check_vma=False)
```

time: 76 us -> 71.8 us (0.945)
  Pallas kernels: 72.3 us -> 67.8 us
    pallas_call x1, Pallas kernels: 72.3 us -> 67.8 us  [local(): pl.pallas_call(kernel, out_shape=(jax.ShapeDtypeStruct((TQ, HQ * HD), bf1...]
where the time goes in v3:
time: 71.8 us; the launch traced here: 71.3 us
  Pallas kernels  67.8 us (94%)
  local copies, waits for them, and re-layouts  2.87 us (4%)
    pallas_call x1, Pallas kernels, local(): pl.pallas_call(kernel, out_shape=(jax.ShapeDtypeStruct((TQ, HQ * HD), bf1...  67.8 us
    unnamed x4, local copies, waits for them, and re-layouts  2.87 us

profile of v3, /device:TPU:24, one launch (start us, length us, event | category | flops | bytes accessed | tf_op | source)
XLA Modules:
  0.0 71.3 jit_solution(3627315476796050411)
XLA Ops:
  0.6 67.8 %shard_map.86 = (bf16[128,4096]{1,0:T(8,128)(2,1)}, f32[1,512]{1,0:T(1,128)}) custom-call(s32[16,16]{1,0:T(8,128)} %dest_ref.1, s32[1,16]{1,0:T(1,128)} %bins_ref.1, bf16[16,8,4096]{2,1,0:T(8,128)(2,1)} %bitcast.7, bf16[16,8,512]{2,1,0:T(8,128)(2,1)} %bitcast.9, bf16[16,8,512]{2,1,0:T(8,128)(2,1)} %bitcast.10, s32[1,1,128]{2,1,0:T(1,128)} %bitcast.13, ...), custom_call_target="tpu_custom_call" | custom-call | tf_op jit(solution)/shard_map/pallas_call | solution.py:385
  68.4 0.0 copy-start
  68.4 2.3 %copy.11 = bf16[1,128,4096]{2,1,0:T(8,128)(2,1)} copy(bf16[1,128,4096]{2,1,0:T(8,128)(2,1)} %bitcast.8) | data formatting | bytes 2097152
  70.7 0.0 copy-done
  70.7 0.6 copy.12
Async XLA Ops:
  68.4 2.3 %copy-start = (f32[1,512]{1,0:T(1,128)S(1)}, f32[1,512]{1,0:T(1,128)}, u32[]{:S(2)}) copy-start(f32[1,512]{1,0:T(1,128)} %get-tuple-element.5) | copy-start | bytes 6148

commit v4 on v3

--- a/solution.py
+++ b/solution.py
@@ -53,10 +53,10 @@
 
 def kernel(
     dest_ref, bins_ref, rq_hbm, rk_hbm, rv_hbm, seg_ref, rw_hbm,
-    out_hbm, hist_ref,
-    rq_ref, rk_ref, rv_ref, rw_ref, qsend, qrecv, ksend, krecv, vsend, vrecv, qs, qe, kbuf, vbuf, out_ref, seg_next,
+    out_ref, hist_ref,
+    rq_ref, rk_ref, rv_ref, rw_ref, qsend, qrecv, ksend, krecv, vsend, vrecv, qs, qe, kbuf, vbuf, seg_next,
     bias, bias_end, hist_a, hist_b,
-    in_sem, out_sem, q_ss, q_rs, k_ss, k_rs, v_ss, v_rs, seg_ss, seg_rs, item_ss, item_rs,
+    in_sem, q_ss, q_rs, k_ss, k_rs, v_ss, v_rs, seg_ss, seg_rs, item_ss, item_rs,
     ha_ss, ha_rs, hb_ss, hb_rs, known,
 ):
     dp = lax.axis_index("dp")
@@ -297,17 +297,12 @@
         bin_of = jnp.where(bin_seg == s, bins_ref[0, s], bin_of)
     hist_a[dp] = jnp.sum(jnp.where(bin_of == bin_lane, reward, 0.0), axis=0, keepdims=True)
 
-    def out_copy(i):
-        at = pl.ds(pl.multiple_of(i * PER * HD, PER * HD), PER * HD)
-        return pltpu.make_async_copy(out_ref.at[:, at], out_hbm.at[:, at], out_sem.at[i])
-
     def heads(i, carry):
         per = PER
         o = attend(qs[pl.ds(i * per, per)].reshape(per * TQ, HD), i // (GROUP // per), bias[...], per, TQ)
         for e in range(per):
             at = pl.ds(pl.multiple_of((i * per + e) * HD, HD), HD)
             out_ref[:, at] = o[e]
-        out_copy(i).start()
         return carry
 
     def hist_copy(buf, ss, rs, axis, me, k):
@@ -367,12 +362,6 @@
 
     lax.fori_loop(0, k_sends, drain_items(0), 0)
     lax.fori_loop(k_sends, k_sends + counted(256, 512), drain_items(16), 0)
-
-    def drain_out(i, carry):
-        out_copy(i).wait()
-        return carry
-
-    lax.fori_loop(0, HQ // PER, drain_out, 0)
 
 
 def local(roll_query, roll_keys, roll_values, pack_dest, segment_ids, reward_bins, reward_weight):
@@ -384,9 +373,9 @@
     most = max(sum(n >= 0 for n in steps) for steps in ROUTES)
     out, hist = pl.pallas_call(
         kernel,
-        out_shape=(jax.ShapeDtypeStruct((TQ, HQ * HD), bf16), jax.ShapeDtypeStruct((1, BINS), f32)),
+        out_shape=(pltpu.VMEM((TQ, HQ * HD), bf16), pltpu.VMEM((1, BINS), f32)),
         in_specs=[smem, smem, hbm, hbm, hbm, vmem, hbm],
-        out_specs=(hbm, vmem),
+        out_specs=(vmem, vmem),
         scratch_shapes=[
             pltpu.VMEM((NB, BLK, HQ * HD), bf16),
             pltpu.VMEM((NB, BLK, HK * HD), bf16),
@@ -402,18 +391,17 @@
             pltpu.VMEM((HK, GROUP * SEGS, HD), bf16),
             pltpu.VMEM((16, HK * TQ + 16, HD), bf16),
             pltpu.VMEM((16, HK * TQ, HD), bf16),
-            pltpu.VMEM((TQ, HQ * HD), bf16),
             pltpu.VMEM((1, TQ), i32),
             pltpu.VMEM((TQ, WIN * TQ), f32),
             pltpu.VMEM((SEGS, WIN * TQ), f32),
             pltpu.VMEM((16, 1, BINS), f32),
             pltpu.VMEM((16, 1, BINS), f32),
-            dma((4,)), dma((HQ // PER,)), dma((16,)), dma((16,)), dma((16,)), dma((16,)), dma((16,)), dma((16,)),
+            dma((4,)), dma((16,)), dma((16,)), dma((16,)), dma((16,)), dma((16,)), dma((16,)),
             dma, dma, dma((most,)), dma((32,)), dma((16,)), dma((16,)), dma((16,)), dma((16,)),
             pltpu.SemaphoreType.REGULAR((4,)),
         ],
         compiler_params=pltpu.CompilerParams(
-            collective_id=0, has_side_effects=True, vmem_limit_bytes=60 * 1024 * 1024
+            collective_id=0, has_side_effects=True, vmem_limit_bytes=56 * 1024 * 1024
         ),
     )(
         pack_dest,

time: 71.8 us -> 69.6 us (0.969)
  local copies, waits for them, and re-layouts: 2.87 us -> 1.55 us
  Pallas kernels: 67.8 us -> 66.9 us
    unnamed x4 -> x2, local copies, waits for them, and re-layouts: 2.87 us -> 1.55 us
    pallas_call x1, Pallas kernels: 67.8 us -> 66.9 us  [local(): pl.pallas_call(kernel, out_shape=(pltpu.VMEM((TQ, HQ * HD), bf16), pltpu....]
where the time goes in v4:
time: 69.6 us; the launch traced here: 69.1 us
  Pallas kernels  66.9 us (96%)
  local copies, waits for them, and re-layouts  1.55 us (2%)
    pallas_call x1, Pallas kernels, local(): pl.pallas_call(kernel, out_shape=(pltpu.VMEM((TQ, HQ * HD), bf16), pltpu....  66.9 us
    unnamed x2, local copies, waits for them, and re-layouts  1.55 us

profile of v4, /device:TPU:24, one launch (start us, length us, event | category | flops | bytes accessed | tf_op | source)
XLA Modules:
  0.0 69.1 jit_solution(4466758055581289746)
XLA Ops:
  0.6 66.9 %shard_map.86 = (bf16[128,4096]{1,0:T(8,128)(2,1)S(1)}, f32[1,512]{1,0:T(1,128)S(1)}) custom-call(s32[16,16]{1,0:T(8,128)} %dest_ref.1, s32[1,16]{1,0:T(1,128)} %bins_ref.1, bf16[16,8,4096]{2,1,0:T(8,128)(2,1)} %bitcast.9, bf16[16,8,512]{2,1,0:T(8,128)(2,1)} %bitcast.10, bf16[16,8,512]{2,1,0:T(8,128)(2,1)} %bitcast.11, s32[1,1,128]{2,1,0:T(1,128)} %bitcast.13, ...), custom_call_target="tpu_custom_call" | custom-call | tf_op jit(solution)/shard_map/pallas_call | solution.py:374
  67.5 1.0 %copy.11 = bf16[1,128,4096]{2,1,0:T(8,128)(2,1)} copy(bf16[1,128,4096]{2,1,0:T(8,128)(2,1)S(1)} %bitcast.7) | data formatting | bytes 2097152
  68.5 0.6 copy.12

commit v5 on v4

--- a/solution.py
+++ b/solution.py
@@ -52,9 +52,9 @@
 
 
 def kernel(
-    dest_ref, bins_ref, rq_hbm, rk_hbm, rv_hbm, seg_ref, rw_hbm,
+    dest_hbm, bins_hbm, rq_hbm, rk_hbm, rv_hbm, seg_hbm, rw_hbm,
     out_ref, hist_ref,
-    rq_ref, rk_ref, rv_ref, rw_ref, qsend, qrecv, ksend, krecv, vsend, vrecv, qs, qe, kbuf, vbuf, seg_next,
+    dest_ref, bins_ref, seg_ref, rq_ref, rk_ref, rv_ref, rw_ref, qsend, qrecv, ksend, krecv, vsend, vrecv, qs, qe, kbuf, vbuf, seg_next,
     bias, bias_end, hist_a, hist_b,
     in_sem, q_ss, q_rs, k_ss, k_rs, v_ss, v_rs, seg_ss, seg_rs, item_ss, item_rs,
     ha_ss, ha_rs, hb_ss, hb_rs, known,
@@ -66,7 +66,10 @@
     loads = [
         pltpu.make_async_copy(src, dst, in_sem.at[i])
         for i, (src, dst) in enumerate(
-            ((rk_hbm, rk_ref), (rv_hbm, rv_ref), (rq_hbm, rq_ref), (rw_hbm, rw_ref))
+            (
+                (dest_hbm, dest_ref), (rk_hbm, rk_ref), (rv_hbm, rv_ref), (seg_hbm, seg_ref),
+                (bins_hbm, bins_ref), (rq_hbm, rq_ref), (rw_hbm, rw_ref),
+            )
         )
     ]
     barrier = pltpu.get_barrier_semaphore()
@@ -116,8 +119,9 @@
     v_copy, v_start, v_wait = exchange(vsend, vrecv, v_ss, v_rs)
     q_copy, q_start, q_wait = exchange(qsend, qrecv, q_ss, q_rs)
     loads[0].wait()
+    loads[1].wait()
     fill(rk_ref, ksend)
-    loads[1].wait()
+    loads[2].wait()
     fill(rv_ref, vsend)
     pl.semaphore_wait(barrier, 18 + jnp.where(ctx == 8, 1, 0))
     lax.fori_loop(1, 16, k_start, 0)
@@ -132,6 +136,8 @@
     def heard(r):
         pl.semaphore_wait(known.at[r], 3)
 
+    loads[3].wait()
+    loads[4].wait()
     seg_copy = remote(seg_ref.at[0], seg_next, seg_ss, seg_rs, {"ctx": (ctx + 15) % 16})
     spread(0)
 
@@ -139,9 +145,9 @@
     def _():
         seg_copy.start()
 
-    loads[2].wait()
+    loads[5].wait()
     fill(rq_ref, qsend)
-    loads[3].wait()
+    loads[6].wait()
     heard(0)
     spread(1)
 
@@ -325,10 +331,10 @@
         return jnp.sum(buf[...], axis=0)
 
     hist_start(hist_a, ha_ss, ha_rs, "dp", dp)
-    lax.fori_loop(0, HALF, heads, 0)
+    lax.fori_loop(0, HALF, heads, 0, unroll=2)
     hist_b[ctx] = hist_total(hist_a, ha_ss, ha_rs, "dp", dp)
     hist_start(hist_b, hb_ss, hb_rs, "ctx", ctx)
-    lax.fori_loop(HALF, HQ // PER, heads, 0)
+    lax.fori_loop(HALF, HQ // PER, heads, 0, unroll=2)
     hist_ref[...] = hist_total(hist_b, hb_ss, hb_rs, "ctx", ctx)
 
     def drain(k, carry):
@@ -366,7 +372,6 @@
 
 def local(roll_query, roll_keys, roll_values, pack_dest, segment_ids, reward_bins, reward_weight):
     vmem = pl.BlockSpec(memory_space=pltpu.VMEM)
-    smem = pl.BlockSpec(memory_space=pltpu.SMEM)
     hbm = pl.BlockSpec(memory_space=pltpu.HBM)
     bf16, f32, i32 = jnp.bfloat16, jnp.float32, jnp.int32
     dma = pltpu.SemaphoreType.DMA
@@ -374,9 +379,12 @@
     out, hist = pl.pallas_call(
         kernel,
         out_shape=(pltpu.VMEM((TQ, HQ * HD), bf16), pltpu.VMEM((1, BINS), f32)),
-        in_specs=[smem, smem, hbm, hbm, hbm, vmem, hbm],
+        in_specs=[hbm] * 7,
         out_specs=(vmem, vmem),
         scratch_shapes=[
+            pltpu.SMEM((16, NB), i32),
+            pltpu.SMEM((1, SEGS), i32),
+            pltpu.VMEM((1, 1, TQ), i32),
             pltpu.VMEM((NB, BLK, HQ * HD), bf16),
             pltpu.VMEM((NB, BLK, HK * HD), bf16),
             pltpu.VMEM((NB, BLK, HK * HD), bf16),
@@ -396,7 +404,7 @@
             pltpu.VMEM((SEGS, WIN * TQ), f32),
             pltpu.VMEM((16, 1, BINS), f32),
             pltpu.VMEM((16, 1, BINS), f32),
-            dma((4,)), dma((16,)), dma((16,)), dma((16,)), dma((16,)), dma((16,)), dma((16,)),
+            dma((7,)), dma((16,)), dma((16,)), dma((16,)), dma((16,)), dma((16,)), dma((16,)),
             dma, dma, dma((most,)), dma((32,)), dma((16,)), dma((16,)), dma((16,)), dma((16,)),
             pltpu.SemaphoreType.REGULAR((4,)),
         ],

time: 69.6 us -> 67.5 us (0.970); the launches traced: 69.1 us -> 66.2 us
  Pallas kernels: 66.9 us -> 64 us
    pallas_call x1, Pallas kernels: 66.9 us -> 64 us  [local(): pl.pallas_call(kernel, out_shape=(pltpu.VMEM((TQ, HQ * HD), bf16), pltpu....]
where the time goes in v5:
time: 67.5 us; the launch traced here: 66.2 us
  Pallas kernels  64 us (95%)
  local copies, waits for them, and re-layouts  1.55 us (2%)
    pallas_call x1, Pallas kernels, local(): pl.pallas_call(kernel, out_shape=(pltpu.VMEM((TQ, HQ * HD), bf16), pltpu....  64 us
    unnamed x2, local copies, waits for them, and re-layouts  1.55 us

profile of v5, /device:TPU:24, one launch (start us, length us, event | category | flops | bytes accessed | tf_op | source)
XLA Modules:
  0.0 66.2 jit_solution(8719266083949038834)
XLA Ops:
  0.6 64.0 %shard_map.86 = (bf16[128,4096]{1,0:T(8,128)(2,1)S(1)}, f32[1,512]{1,0:T(1,128)S(1)}) custom-call(s32[16,16]{1,0:T(8,128)} %dest_hbm.1, s32[1,16]{1,0:T(1,128)} %bins_hbm.1, bf16[16,8,4096]{2,1,0:T(8,128)(2,1)} %bitcast.9, bf16[16,8,512]{2,1,0:T(8,128)(2,1)} %bitcast.10, bf16[16,8,512]{2,1,0:T(8,128)(2,1)} %bitcast.11, s32[1,1,128]{2,1,0:T(1,128)} %bitcast.13, ...), custom_call_target="tpu_custom_call" | custom-call | tf_op jit(solution)/shard_map/pallas_call | solution.py:379
  64.7 1.0 %copy.11 = bf16[1,128,4096]{2,1,0:T(8,128)(2,1)} copy(bf16[1,128,4096]{2,1,0:T(8,128)(2,1)S(1)} %bitcast.7) | data formatting | bytes 2097152
  65.7 0.6 copy.12

commit v6 on v5

--- a/solution.py
+++ b/solution.py
@@ -54,7 +54,7 @@
 def kernel(
     dest_hbm, bins_hbm, rq_hbm, rk_hbm, rv_hbm, seg_hbm, rw_hbm,
     out_ref, hist_ref,
-    dest_ref, bins_ref, seg_ref, rq_ref, rk_ref, rv_ref, rw_ref, qsend, qrecv, ksend, krecv, vsend, vrecv, qs, qe, kbuf, vbuf, seg_next,
+    dest_ref, bins_ref, source, seg_ref, rq_ref, rk_ref, rv_ref, rw_ref, qsend, qrecv, ksend, krecv, vsend, vrecv, qs, qe, kbuf, vbuf, seg_next,
     bias, bias_end, hist_a, hist_b,
     in_sem, q_ss, q_rs, k_ss, k_rs, v_ss, v_rs, seg_ss, seg_rs, item_ss, item_rs,
     ha_ss, ha_rs, hb_ss, hb_rs, known,
@@ -78,7 +78,7 @@
         pl.semaphore_signal(barrier, inc=1, device_id={"dp": (dp + k) % 16}, device_id_type=MESH)
         return carry
 
-    lax.fori_loop(1, 16, greet, 0)
+    lax.fori_loop(1, 16, greet, 0, unroll=5)
     for to in near:
         pl.semaphore_signal(barrier, inc=1, device_id={"ctx": to}, device_id_type=MESH)
 
@@ -124,7 +124,7 @@
     loads[2].wait()
     fill(rv_ref, vsend)
     pl.semaphore_wait(barrier, 18 + jnp.where(ctx == 8, 1, 0))
-    lax.fori_loop(1, 16, k_start, 0)
+    lax.fori_loop(1, 16, k_start, 0, unroll=5)
     lax.fori_loop(1, 16, v_start, 0)
     krecv[dp] = ksend[dp]
     vrecv[dp] = vsend[dp]
@@ -151,15 +151,15 @@
     heard(0)
     spread(1)
 
-    def source_of(j):
+    for j in range(NB):
         src = jnp.int32(0)
         for s in range(16):
             src = jnp.where(dest_ref[s, j] == dp, s, src)
-        return src
+        source[j] = src
 
     def rows_of(recv, jj):
-        top = recv[source_of(2 * jj)].astype(jnp.float32)
-        low = recv[source_of(2 * jj + 1)].astype(jnp.float32)
+        top = recv[source[2 * jj]].astype(jnp.float32)
+        low = recv[source[2 * jj + 1]].astype(jnp.float32)
         return jnp.concatenate([top, low], axis=0).astype(jnp.bfloat16)
 
     def pack(recv, buf):
@@ -170,7 +170,7 @@
                 buf[ctx, at, :] = rows[:, g * HD : (g + 1) * HD]
             return carry
 
-        lax.fori_loop(0, NB // 2, body, 0)
+        lax.fori_loop(0, NB // 2, body, 0, unroll=4)
 
     def item_copy(item, to, slot):
         buf = (kbuf, vbuf)[item // 16].at[item % 16]
@@ -192,7 +192,7 @@
     first = [next((i for i, n in enumerate(steps) if n < 0), len(steps)) for steps in ROUTES]
     seg_row = seg_ref[0]
     kbuf[ctx, HK * TQ :, :] = jnp.broadcast_to(seg_row.astype(jnp.float32), (16, TQ)).astype(jnp.bfloat16)
-    lax.fori_loop(1, 16, k_wait, 0)
+    lax.fori_loop(1, 16, k_wait, 0, unroll=5)
     pack(krecv, kbuf)
     for c, steps in enumerate(ROUTES):
         @pl.when(ctx == c)
@@ -319,7 +319,7 @@
             hist_copy(buf, ss, rs, axis, me, k).start()
             return carry
 
-        lax.fori_loop(1, 16, start, 0)
+        lax.fori_loop(1, 16, start, 0, unroll=5)
 
     def hist_total(buf, ss, rs, axis, me):
         def wait(k, carry):
@@ -327,7 +327,7 @@
             remote(buf.at[s], buf.at[s], ss.at[k], rs.at[s], {axis: s}).wait_recv()
             return carry
 
-        lax.fori_loop(1, 16, wait, 0)
+        lax.fori_loop(1, 16, wait, 0, unroll=5)
         return jnp.sum(buf[...], axis=0)
 
     hist_start(hist_a, ha_ss, ha_rs, "dp", dp)
@@ -335,14 +335,11 @@
     hist_b[ctx] = hist_total(hist_a, ha_ss, ha_rs, "dp", dp)
     hist_start(hist_b, hb_ss, hb_rs, "ctx", ctx)
     lax.fori_loop(HALF, HQ // PER, heads, 0, unroll=2)
-    hist_ref[...] = hist_total(hist_b, hb_ss, hb_rs, "ctx", ctx)
-
     def drain(k, carry):
         k_copy(k).wait_send()
         v_copy(k).wait_send()
         q_copy(k).wait_send()
         hist_copy(hist_a, ha_ss, ha_rs, "dp", dp, k).wait_send()
-        hist_copy(hist_b, hb_ss, hb_rs, "ctx", ctx, k).wait_send()
         return carry
 
     lax.fori_loop(1, 16, drain, 0)
@@ -368,6 +365,14 @@
 
     lax.fori_loop(0, k_sends, drain_items(0), 0)
     lax.fori_loop(k_sends, k_sends + counted(256, 512), drain_items(16), 0)
+
+    hist_ref[...] = hist_total(hist_b, hb_ss, hb_rs, "ctx", ctx)
+
+    def drain_last(k, carry):
+        hist_copy(hist_b, hb_ss, hb_rs, "ctx", ctx, k).wait_send()
+        return carry
+
+    lax.fori_loop(1, 16, drain_last, 0, unroll=5)
 
 
 def local(roll_query, roll_keys, roll_values, pack_dest, segment_ids, reward_bins, reward_weight):
@@ -384,6 +389,7 @@
         scratch_shapes=[
             pltpu.SMEM((16, NB), i32),
             pltpu.SMEM((1, SEGS), i32),
+            pltpu.SMEM((NB,), i32),
             pltpu.VMEM((1, 1, TQ), i32),
             pltpu.VMEM((NB, BLK, HQ * HD), bf16),
             pltpu.VMEM((NB, BLK, HK * HD), bf16),

time: 67.5 us -> 66.5 us (0.985); the launches traced: 66.2 us -> 66 us
  no operation moved by 1% of the time
where the time goes in v6:
time: 66.5 us; the launch traced here: 66 us
  Pallas kernels  63.8 us (96%)
  local copies, waits for them, and re-layouts  1.55 us (2%)
    pallas_call x1, Pallas kernels, local(): pl.pallas_call(kernel, out_shape=(pltpu.VMEM((TQ, HQ * HD), bf16), pltpu....  63.8 us
    unnamed x2, local copies, waits for them, and re-layouts  1.55 us

profile of v6, /device:TPU:24, one launch (start us, length us, event | category | flops | bytes accessed | tf_op | source)
XLA Modules:
  0.0 66.0 jit_solution(9109193296973252241)
XLA Ops:
  0.6 63.8 %shard_map.86 = (bf16[128,4096]{1,0:T(8,128)(2,1)S(1)}, f32[1,512]{1,0:T(1,128)S(1)}) custom-call(s32[16,16]{1,0:T(8,128)} %dest_hbm.1, s32[1,16]{1,0:T(1,128)} %bins_hbm.1, bf16[16,8,4096]{2,1,0:T(8,128)(2,1)} %bitcast.9, bf16[16,8,512]{2,1,0:T(8,128)(2,1)} %bitcast.10, bf16[16,8,512]{2,1,0:T(8,128)(2,1)} %bitcast.11, s32[1,1,128]{2,1,0:T(1,128)} %bitcast.13, ...), custom_call_target="tpu_custom_call" | custom-call | tf_op jit(solution)/shard_map/pallas_call | solution.py:384
  64.4 1.0 %copy.11 = bf16[1,128,4096]{2,1,0:T(8,128)(2,1)} copy(bf16[1,128,4096]{2,1,0:T(8,128)(2,1)S(1)} %bitcast.7) | data formatting | bytes 2097152
  65.4 0.6 copy.12

commit v7 on v6

--- a/solution.py
+++ b/solution.py
@@ -125,7 +125,7 @@
     fill(rv_ref, vsend)
     pl.semaphore_wait(barrier, 18 + jnp.where(ctx == 8, 1, 0))
     lax.fori_loop(1, 16, k_start, 0, unroll=5)
-    lax.fori_loop(1, 16, v_start, 0)
+    lax.fori_loop(1, 16, v_start, 0, unroll=5)
     krecv[dp] = ksend[dp]
     vrecv[dp] = vsend[dp]
 
@@ -192,25 +192,7 @@
     first = [next((i for i, n in enumerate(steps) if n < 0), len(steps)) for steps in ROUTES]
     seg_row = seg_ref[0]
     kbuf[ctx, HK * TQ :, :] = jnp.broadcast_to(seg_row.astype(jnp.float32), (16, TQ)).astype(jnp.bfloat16)
-    lax.fori_loop(1, 16, k_wait, 0, unroll=5)
-    pack(krecv, kbuf)
-    for c, steps in enumerate(ROUTES):
-        @pl.when(ctx == c)
-        def _():
-            run_steps(c, [n for n in steps[: first[c]] if n < 256])
-
-    lax.fori_loop(1, 16, v_wait, 0)
-    pack(vrecv, vbuf)
-    for c, steps in enumerate(ROUTES):
-        @pl.when(ctx == c)
-        def _():
-            run_steps(c, [n for n in steps[: first[c]] if n >= 256])
-
-    lax.fori_loop(1, 16, q_start, 0)
-    qrecv[dp] = qsend[dp]
-    heard(1)
-    spread(2)
-    for c, steps in enumerate(ROUTES):
+    for c, steps in enumerate(ROUTES[: WIN - 1]):
         @pl.when(ctx == c)
         def _():
             for b in range(c + 1, WIN):
@@ -218,6 +200,28 @@
                     kbuf[b] = jnp.zeros((HK * TQ + 16, HD), jnp.bfloat16)
                 if -1 - (16 + b) not in steps:
                     vbuf[b] = jnp.zeros((HK * TQ, HD), jnp.bfloat16)
+
+    lax.fori_loop(1, 16, k_wait, 0, unroll=5)
+    pack(krecv, kbuf)
+    for c, steps in enumerate(ROUTES):
+        @pl.when(ctx == c)
+        def _():
+            run_steps(c, [n for n in steps[: first[c]] if n < 256])
+
+    lax.fori_loop(1, 16, v_wait, 0, unroll=5)
+    pack(vrecv, vbuf)
+    for c, steps in enumerate(ROUTES):
+        @pl.when(ctx == c)
+        def _():
+            run_steps(c, [n for n in steps[: first[c]] if n >= 256])
+
+    lax.fori_loop(1, 16, q_start, 0, unroll=5)
+    qrecv[dp] = qsend[dp]
+    heard(1)
+    spread(2)
+    for c, steps in enumerate(ROUTES):
+        @pl.when(ctx == c)
+        def _():
             run_steps(c, steps[first[c] : CUTS[c]])
 
     heard(2)
@@ -231,7 +235,7 @@
             qs[h, at, :] = rows[:, h * HD : (h + 1) * HD]
         return carry
 
-    lax.fori_loop(0, NB // 2, pack_q, 0)
+    lax.fori_loop(0, NB // 2, pack_q, 0, unroll=2)
 
     @pl.when(ctx < 15)
     def _():

time: 66.5 us -> 66.5 us (level)
  no operation moved by 1% of the time
where the time goes in v7:
time: 66.5 us; the launch traced here: 66 us
  Pallas kernels  63.8 us (96%)
  local copies, waits for them, and re-layouts  1.55 us (2%)
    pallas_call x1, Pallas kernels, local(): pl.pallas_call(kernel, out_shape=(pltpu.VMEM((TQ, HQ * HD), bf16), pltpu....  63.8 us
    unnamed x2, local copies, waits for them, and re-layouts  1.55 us

profile of v7, /device:TPU:24, one launch (start us, length us, event | category | flops | bytes accessed | tf_op | source)
XLA Modules:
  0.0 66.0 jit_solution(6112791593867235222)
XLA Ops:
  0.6 63.8 %shard_map.86 = (bf16[128,4096]{1,0:T(8,128)(2,1)S(1)}, f32[1,512]{1,0:T(1,128)S(1)}) custom-call(s32[16,16]{1,0:T(8,128)} %dest_hbm.1, s32[1,16]{1,0:T(1,128)} %bins_hbm.1, bf16[16,8,4096]{2,1,0:T(8,128)(2,1)} %bitcast.9, bf16[16,8,512]{2,1,0:T(8,128)(2,1)} %bitcast.10, bf16[16,8,512]{2,1,0:T(8,128)(2,1)} %bitcast.11, s32[1,1,128]{2,1,0:T(1,128)} %bitcast.13, ...), custom_call_target="tpu_custom_call" | custom-call | tf_op jit(solution)/shard_map/pallas_call | solution.py:388
  64.4 1.0 %copy.11 = bf16[1,128,4096]{2,1,0:T(8,128)(2,1)} copy(bf16[1,128,4096]{2,1,0:T(8,128)(2,1)S(1)} %bitcast.7) | data formatting | bytes 2097152
  65.4 0.6 copy.12
